TPU v7x, 128 devices: a whole 4x4x4 slice. The times are simulated.
128 devices in a mesh: node: 32 (over z, x, core), mp: 4 (over y).
Axes of the slice: x: 4, y: 4, z: 4, core: 2. Of those that a mesh axis runs over, the one named last changes fastest.
Arguments:
- queries: bfloat16 [128, 64, 128], P('node', 'mp'), may hold values from -8 to 8
- root_keys: bfloat16 [16384, 8, 128], P('node', 'mp'), may hold values from -6 to 6
- root_values: bfloat16 [16384, 8, 128], P('node', 'mp'), may hold values from -6 to 6
- mid_keys: bfloat16 [32, 1024, 8, 128], P('node', None, 'mp'), may hold values from -6 to 6
- mid_values: bfloat16 [32, 1024, 8, 128], P('node', None, 'mp'), may hold values from -6 to 6
- leaf_keys: bfloat16 [128, 256, 8, 128], P('node', None, 'mp'), may hold values from -6 to 6
- leaf_values: bfloat16 [128, 256, 8, 128], P('node', None, 'mp'), may hold values from -6 to 6
- mid_length: int32 [32], replicated, may hold values from 1 to 1024
- leaf_length: int32 [128], P('node'), may hold values from 1 to 256
- branch_mid: int32 [128, 1], replicated, may hold values from 0 to 31; in each aligned block of 128 rows (0 to 127, 128 to 255, ...) at most 8 rows name the same one
- residual: bfloat16 [128, 8192], P(None, 'node'), may hold values from -6 to 6
- norm_gain: float32 [8192], P('node'), may hold values from 0.5 to 1.5
- out_weight: bfloat16 [8192, 8192], P('mp', 'node'), may hold values from -0.0625 to 0.0625
- gate_weight: bfloat16 [8192, 28672], P('node', 'mp'), may hold values from -0.0625 to 0.0625
- up_weight: bfloat16 [8192, 28672], P('node', 'mp'), may hold values from -0.0625 to 0.0625
- down_weight: bfloat16 [28672, 8192], P('mp', 'node'), may hold values from -0.03125 to 0.03125
Outputs:
- layer_out: bfloat16 [128, 8192], P('mp', 'node')
Inputs may be any that keep to these rules, and one draw needn't show every extreme that they name: `branch_mid`: every inner tree node lies on the path of 1 to 8 branches, and some node on exactly 8.
All inputs are finite; a program needn't handle non-finite values.
Results may differ from a plain program's by a relative error of at most 0.015.
Values may be sent and summed in bfloat16 or wider, within the bound.
No kernel may reach another device: no remote copies, remote signals or barrier semaphores. Data moves between devices by JAX's collectives and lax.ppermute only.
A program may use at most 64 MiB of HBM per device.

v0:
```python
import jax
import jax.numpy as jnp
from jax import lax
from jax.sharding import PartitionSpec as P

D = 8192
CAP = 8


masked_score = -1e30
norm_eps = 1e-05


def copy_for_each(x, axis):
    copies = jnp.broadcast_to(x, (lax.axis_size(axis), *x.shape))
    return lax.all_to_all(copies, axis, split_axis=0, concat_axis=0, tiled=True)


def in_order(parts, dim):
    dims = list(parts.shape[1:])
    dims[dim] *= parts.shape[0]
    return jnp.moveaxis(parts, 0, dim).reshape(dims)


def gather_directly(x, axis, dim):
    parts = copy_for_each(x, axis)
    return in_order(parts, dim)


def sent_together(arrays, axis, split_dim, concat_dim, along):
    columns = [a.reshape(*a.shape[:along], -1) for a in arrays]
    both = jnp.concatenate(columns, axis=along)
    result, at, finished = (
        lax.all_to_all(both, axis, split_axis=split_dim, concat_axis=concat_dim, tiled=True),
        0,
        [],
    )
    for a, column in zip(arrays, columns):
        piece = result[..., at : at + column.shape[along]]
        finished.append(piece.reshape(*piece.shape[:along], *a.shape[along:]))
        at += column.shape[along]
    return tuple(finished)


def taken_together(x, axis):
    everything = copy_for_each(x, axis)
    return jnp.sum(everything.astype(jnp.float32), axis=0)


def over_copies(x, axis):
    everything = copy_for_each(x, axis)
    return jnp.sum(everything, axis=0)


def in_blocks(x, dim, size):
    dims = x.shape
    parts = x.reshape(*dims[:dim], size, dims[dim] // size, *dims[dim + 1 :])
    return jnp.moveaxis(parts, dim, 0)


def sum_at_owner(x, axis, dim):
    parts = in_blocks(x, dim, lax.axis_size(axis))
    arrived = lax.all_to_all(parts, axis, split_axis=0, concat_axis=0, tiled=True)
    return arrived.astype(jnp.float32).sum(axis=0)


def partial_scores(grouped, key_block, value_block, usable, scaling):
    scores = (
        jnp.einsum("bkgd,lkd->bkgl", grouped, key_block, preferred_element_type=jnp.float32)
        * scaling
    )
    masking = usable[:, None, None, :]
    scores = jnp.where(masking, scores, masked_score)
    highest = jnp.max(scores, axis=-1)
    weights = jnp.where(masking, jnp.exp(scores - highest[..., None]), 0.0)
    weighted = jnp.einsum(
        "bkgl,lkd->bkgd",
        weights.astype(jnp.bfloat16),
        value_block,
        preferred_element_type=jnp.float32,
    )
    return (highest, jnp.sum(weights, axis=-1), weighted)


def combine_parts(earlier, later):
    highest = jnp.maximum(earlier[0], later[0])
    first_factor = jnp.exp(earlier[0] - highest)
    second_factor = jnp.exp(later[0] - highest)
    totals = earlier[1] * first_factor + later[1] * second_factor
    weighted = earlier[2] * first_factor[..., None] + later[2] * second_factor[..., None]
    return (highest, totals, weighted)


def on_device(
    queries,
    root_keys,
    root_values,
    mid_keys,
    mid_values,
    leaf_keys,
    leaf_values,
    mid_length,
    leaf_length,
    branch_mid,
    residual,
    norm_gain,
    out_weight,
    gate_weight,
    up_weight,
    down_weight,
):
    owned = queries.shape[0]
    local_heads = queries.shape[1]
    head_size = queries.shape[2]
    local_groups = root_keys.shape[1]
    group_size = local_heads // local_groups
    scaling = head_size ** (-0.5)
    node_count = lax.axis_size("node")
    gathered = gather_directly(queries, "node", 0)
    every_branch = gathered.shape[0]
    grouped = gathered.reshape(every_branch, local_groups, group_size, head_size)
    root_usable = jnp.ones((every_branch, root_keys.shape[0]), dtype=bool)
    root_part = partial_scores(grouped, root_keys, root_values, root_usable, scaling)
    local_mids = mid_keys.shape[0]
    node_ids = lax.axis_index("node") * local_mids + jnp.arange(local_mids, dtype=jnp.int32)
    routing = branch_mid[:, 0]
    matching = routing[None, :] == node_ids[:, None]
    ranking = jnp.cumsum(matching.astype(jnp.int32), axis=1) - 1
    selected = matching[:, None, :] & (
        ranking[:, None, :] == jnp.arange(CAP, dtype=jnp.int32)[None, :, None]
    )
    picked = jnp.einsum(
        "ncb,bkgd->nckgd",
        selected.astype(jnp.bfloat16),
        grouped,
        preferred_element_type=jnp.float32,
    ).astype(jnp.bfloat16)
    slot_index = jnp.arange(mid_keys.shape[1])

    def node_partial(inputs):
        node_queries, node_keys, node_values, node_id = inputs
        usable = jnp.broadcast_to(
            slot_index[None, :] < mid_length[node_id], (CAP, slot_index.shape[0])
        )
        return partial_scores(node_queries, node_keys, node_values, usable, scaling)

    node_high, node_totals, node_weighted = lax.map(
        node_partial, (picked, mid_keys, mid_values, node_ids)
    )
    chosen = selected.astype(jnp.float32)
    covered = jnp.sum(chosen, axis=(0, 1))
    back_high = (
        jnp.einsum("ncb,nckg->bkg", chosen, node_high, precision=lax.Precision.HIGHEST)
        + ((1.0 - covered) * masked_score)[:, None, None]
    )
    back_totals = jnp.einsum("ncb,nckg->bkg", chosen, node_totals, precision=lax.Precision.HIGHEST)
    back_weighted = jnp.einsum(
        "ncb,nckgd->bkgd", chosen, node_weighted, precision=lax.Precision.HIGHEST
    )
    shared_part = combine_parts(root_part, (back_high, back_totals, back_weighted))
    peaks, totals, weighted = sent_together(
        (shared_part[0], shared_part[1], shared_part[2]), "node", 0, 0, 3
    )
    peaks = peaks.reshape(node_count, owned, local_groups, group_size)
    totals = totals.reshape(node_count, owned, local_groups, group_size)
    weighted = weighted.reshape(node_count, owned, local_groups, group_size, head_size)
    highest = jnp.max(peaks, axis=0)
    factor = jnp.exp(peaks - highest[None])
    merged = (
        highest,
        jnp.sum(totals * factor, axis=0),
        jnp.sum(weighted * factor[..., None], axis=0),
    )
    own_grouped = queries.reshape(owned, local_groups, group_size, head_size)
    leaf_scores = (
        jnp.einsum("bkgd,blkd->bkgl", own_grouped, leaf_keys, preferred_element_type=jnp.float32)
        * scaling
    )
    leaf_usable = (jnp.arange(leaf_keys.shape[1])[None, :] < leaf_length[:, None])[:, None, None, :]
    leaf_scores = jnp.where(leaf_usable, leaf_scores, masked_score)
    leaf_peak = jnp.max(leaf_scores, axis=-1)
    leaf_weights = jnp.where(leaf_usable, jnp.exp(leaf_scores - leaf_peak[..., None]), 0.0)
    leaf_weighted = jnp.einsum(
        "bkgl,blkd->bkgd",
        leaf_weights.astype(jnp.bfloat16),
        leaf_values,
        preferred_element_type=jnp.float32,
    )
    final_part = combine_parts(merged, (leaf_peak, jnp.sum(leaf_weights, axis=-1), leaf_weighted))
    attended = (
        (final_part[2] / final_part[1][..., None])
        .reshape(owned, local_heads * head_size)
        .astype(jnp.bfloat16)
    )
    projected = jnp.dot(
        gather_directly(attended, "node", 0), out_weight, preferred_element_type=jnp.float32
    )
    projected = taken_together(projected.astype(jnp.bfloat16), "mp").astype(jnp.float32)
    stream = residual.astype(jnp.float32) + projected
    squares = over_copies(jnp.sum(stream * stream, axis=1), "node")
    normed = (stream * lax.rsqrt(squares[:, None] / D + norm_eps) * norm_gain[None, :]).astype(
        jnp.bfloat16
    )
    out_rows = every_branch // lax.axis_size("mp")
    gate, upward = (
        lax.psum(
            jnp.dot(normed, gate_weight, preferred_element_type=jnp.float32).astype(jnp.bfloat16),
            "node",
        ).astype(jnp.float32),
        lax.psum(
            jnp.dot(normed, up_weight, preferred_element_type=jnp.float32).astype(jnp.bfloat16),
            "node",
        ).astype(jnp.float32),
    )
    act = (jax.nn.silu(gate) * upward).astype(jnp.bfloat16)
    mlp_rows = sum_at_owner(
        jnp.dot(act, down_weight, preferred_element_type=jnp.float32).astype(jnp.bfloat16), "mp", 0
    )
    stream_rows = lax.dynamic_slice_in_dim(stream, lax.axis_index("mp") * out_rows, out_rows, 0)
    return (stream_rows + mlp_rows).astype(jnp.bfloat16)


def solution(mesh):
    in_specs = (
        P("node", "mp", None),
        P("node", "mp", None),
        P("node", "mp", None),
        P("node", None, "mp", None),
        P("node", None, "mp", None),
        P("node", None, "mp", None),
        P("node", None, "mp", None),
        P(),
        P("node"),
        P(),
        P(None, "node"),
        P("node"),
        P("mp", "node"),
        P("node", "mp"),
        P("node", "mp"),
        P("mp", "node"),
    )
    out_specs = P("mp", "node")
    return jax.shard_map(
        on_device, mesh=mesh, in_specs=in_specs, out_specs=out_specs, check_vma=False
    )
```

profile of v0, /device:TPU:1, one launch (start us, length us, event | category | flops | bytes accessed | tf_op | source)
XLA Modules:
  0.0 251.8 jit_solution(14674612298234701820)
XLA Ops:
  6.5 0.0 copy-start
  6.5 0.8 copy.121
  7.4 1.0 broadcast_in_dim.104
  8.4 9.4 %all-to-all-start = ((bf16[32,4,16,128]{3,1,2,0:T(4,128)(2,1)}), bf16[32,4,16,128]{3,1,2,0:T(4,128)(2,1)S(1)}, u32[]{:S(2)}, u32[]{:S(2)}) async-start(bf16[32,4,16,128]{3,1,2,0:T(4,128)(2,1)} %broadcast_in_dim.104), calls=%async_computation | async-start | bytes 1048576 | tf_op jit(solution)/shard_map/all_to_all | solution.py:16
  17.9 0.7 compare_bitcast_fusion
  18.5 0.1 copy.124
  18.6 0.2 reduce-window.7
  18.8 1.2 dynamic_slice.18
  20.0 0.6 iota_compare_fusion.2
  20.7 0.1 add_reduce_fusion
  20.8 8.6 %all-to-all-done = bf16[32,4,16,128]{3,1,2,0:T(4,128)(2,1)S(1)} async-done(((bf16[32,4,16,128]{3,1,2,0:T(4,128)(2,1)}), bf16[32,4,16,128]{3,1,2,0:T(4,128)(2,1)S(1)}, u32[]{:S(2)}, u32[]{:S(2)}) %all-to-all-start) | async-done | bytes 524320 | tf_op jit(solution)/shard_map/all_to_all | solution.py:16
  29.4 0.2 copy.122
  29.6 0.2 convolution_convert_fusion.3
  29.8 1.4 fusion.85
  31.3 0.1 copy.127
  31.3 0.2 fusion.41
  31.6 0.0 copy-done.7
  31.6 0.3 convolution_bitcast_fusion
  31.9 0.1 copy.128
  32.0 1.0 fusion.63
  33.0 0.0 copy-done.2
  33.0 0.0 copy-start.3
  33.0 0.7 bitcast_reduce_fusion
  33.7 0.7 fusion.7
  34.4 0.1 subtract_exponential_fusion.2
  34.6 0.0 copy-done.3
  34.6 1.0 fusion.20
  35.6 0.1 fusion.35
  35.7 0.1 pad_maximum_fusion
  35.8 0.0 copy-start.9
  35.9 0.0 copy-start.5
  35.9 2.0 copy.135
  37.8 4.1 %all-to-all-start.1 = ((f32[128,2,8,130]{3,2,1,0:T(8,128)}), f32[128,2,8,130]{3,2,1,0:T(8,128)S(1)}, u32[]{:S(2)}, u32[]{:S(2)}) async-start(f32[128,2,8,130]{3,2,1,0:T(8,128)} %copy.135), calls=%async_computation.1 | async-start | bytes 4194304 | tf_op jit(solution)/shard_map/all_to_all | solution.py:34
  42.0 0.0 all-reduce.3.cloned.1.call-start
  42.0 0.0 copy-done.9
  42.0 0.1 iota_compare_fusion
  42.1 1.4 fusion.86
  43.5 0.2 fusion.49
  43.6 26.3 %all-to-all-done.1 = f32[128,2,8,130]{3,2,1,0:T(8,128)S(1)} async-done(((f32[128,2,8,130]{3,2,1,0:T(8,128)}), f32[128,2,8,130]{3,2,1,0:T(8,128)S(1)}, u32[]{:S(2)}, u32[]{:S(2)}) %all-to-all-start.1) | async-done | bytes 1064992 | tf_op jit(solution)/shard_map/all_to_all | solution.py:34
  69.9 1.7 fusion.84
  71.6 2.8 %copy.136 = f32[128,2,8,1]{2,0,1,3:T(8,128)S(1)} copy(f32[128,2,8,1]{3,2,1,0:T(8,128)} %get-tuple-element.46) | data formatting | bytes 16384 | tf_op jit(solution)/shard_map/slice | solution.py:39
  74.4 2.8 %copy.144 = f32[128,2,8,1]{2,0,1,3:T(8,128)S(1)} copy(f32[128,2,8,1]{3,2,1,0:T(8,128)} %get-tuple-element.47) | data formatting | bytes 16384 | tf_op jit(solution)/shard_map/slice | solution.py:39
  77.2 0.1 reduce_max.39
  77.2 0.1 multiply_reduce_fusion.2
  77.4 0.1 copy.137
  77.5 0.3 slice.12
  77.8 0.3 multiply_reduce_fusion
  78.2 0.1 copy-done.8
  78.3 0.2 fusion.32
  78.5 0.2 broadcast_in_dim.112
  78.8 16.7 %all_to_all.31 = bf16[32,4,2048]{2,1,0:T(4,128)(2,1)S(1)} all-to-all(bf16[32,4,2048]{2,1,0:T(4,128)(2,1)S(1)} %broadcast_in_dim.112), channel_id=1, replica_groups=mesh['node'=32,'mp'=4] {'node'}, dimensions={0} | all-to-all | bytes 1048576 | tf_op jit(solution)/shard_map/all_to_all | solution.py:16
  95.4 0.1 reshape.287
  95.6 0.3 convolution_convert_fusion.2
  95.9 9.7 %all_to_all.32 = bf16[4,128,256]{2,1,0:T(8,128)(2,1)S(1)} all-to-all(bf16[4,128,256]{2,1,0:T(8,128)(2,1)S(1)} %broadcast_in_dim.113), channel_id=1, replica_groups=mesh['node'=32,'mp'=4] {'mp'}, dimensions={0} | all-to-all | bytes 524288 | tf_op jit(solution)/shard_map/all_to_all | solution.py:16
  105.7 0.1 multiply_reduce_fusion.1
  105.8 12.2 %all_to_all.33 = f32[32,1,128]{2,1,0:T(1,128)S(1)} all-to-all(f32[32,1,128]{2,1,0:T(1,128)S(1)} %broadcast_in_dim.114), channel_id=1, replica_groups=mesh['node'=32,'mp'=4] {'node'}, dimensions={0} | all-to-all | bytes 32768 | tf_op jit(solution)/shard_map/all_to_all | solution.py:16
  118.1 4.1 %convolution_convert_fusion = bf16[128,7168]{1,0:T(8,128)(2,1)} fusion(bf16[256,7168]{1,0:T(8,128)(2,1)} %param.30, f32[128,256]{1,0:T(8,128)S(1)} %get-tuple-element.26, f32[256]{0:T(256)S(1)} %copy-done.6, f32[128]{0:T(128)S(1)} %add_rsqrt_fusion), kind=kOutput, calls=%fused_computation | convolution fusion | flops 470777856 | bytes 5637632 | tf_op jit(solution)/shard_map/dot_general | solution.py:211
  122.2 2.0 convolution_convert_fusion.1
  124.2 0.0 all-reduce.3.cloned.1.call-update
  124.2 106.6 %all-reduce.3.cloned.1.call-done = (bf16[128,7168]{1,0:T(8,128)(2,1)}, bf16[128,7168]{1,0:T(8,128)(2,1)}) async-done(((bf16[128,7168]{1,0:T(8,128)(2,1)}, bf16[128,7168]{1,0:T(8,128)(2,1)}), (bf16[128,7168]{1,0:T(8,128)(2,1)}, bf16[128,7168]{1,0:T(8,128)(2,1)})) %all-reduce.3.cloned.1.call-update) | async-done | bytes 3670032 | tf_op jit(solution)/shard_map/psum | solution.py:210
  230.9 5.0 %fusion.25 = bf16[128,256]{1,0:T(8,128)(2,1)} fusion(bf16[7168,256]{1,0:T(8,128)(2,1)} %param.31, bf16[128,7168]{1,0:T(8,128)(2,1)} %get-tuple-element.23, bf16[128,7168]{1,0:T(8,128)(2,1)} %get-tuple-element.24), kind=kOutput, calls=%fused_computation.24 | convolution fusion | flops 477134848 | bytes 7405568 | tf_op jit(solution)/shard_map/dot_general | solution.py:217
  235.8 4.0 %all-to-all-start.5 = ((bf16[4,32,256]{2,1,0:T(8,128)(2,1)}), bf16[4,32,256]{2,1,0:T(8,128)(2,1)S(1)}, u32[]{:S(2)}, u32[]{:S(2)}) async-start(bf16[4,32,256]{2,1,0:T(8,128)(2,1)} %bitcast.30), calls=%async_computation.5 | async-start | bytes 131072 | tf_op jit(solution)/shard_map/all_to_all | solution.py:63
  239.9 4.5 %all-to-all-done.5 = bf16[4,32,256]{2,1,0:T(8,128)(2,1)S(1)} async-done(((bf16[4,32,256]{2,1,0:T(8,128)(2,1)}), bf16[4,32,256]{2,1,0:T(8,128)(2,1)S(1)}, u32[]{:S(2)}, u32[]{:S(2)}) %all-to-all-start.5) | async-done | bytes 65568 | tf_op jit(solution)/shard_map/all_to_all | solution.py:63
  244.3 0.6 add_convert_fusion
  (26 shorter events, 0.2 us)
Async XLA Ops:
  6.5 89.0 %copy-start = (bf16[2048,256]{1,0:T(8,128)(2,1)S(1)}, bf16[2048,256]{1,0:T(8,128)(2,1)}, u32[]{:S(2)}) copy-start(bf16[2048,256]{1,0:T(8,128)(2,1)} %param.28) | copy-start | bytes 3145732
  6.5 25.0 %copy-start.7 = (bf16[1,1024,2,128]{3,2,1,0:T(2,128)(2,1)S(1)}, bf16[1,1024,2,128]{3,2,1,0:T(2,128)(2,1)}, u32[]{:S(2)}) copy-start(bf16[1,1024,2,128]{3,2,1,0:T(2,128)(2,1)} %param.20) | copy-start | bytes 1572868
  7.4 25.6 %copy-start.2 = (bf16[512,2,128]{2,1,0:T(2,128)(2,1)S(1)}, bf16[512,2,128]{2,1,0:T(2,128)(2,1)}, u32[]{:S(2)}) copy-start(bf16[512,2,128]{2,1,0:T(2,128)(2,1)} %param.17) | copy-start | bytes 786436
  8.4 21.0 %all-to-all-start = ((bf16[32,4,16,128]{3,1,2,0:T(4,128)(2,1)}), bf16[32,4,16,128]{3,1,2,0:T(4,128)(2,1)S(1)}, u32[]{:S(2)}, u32[]{:S(2)}) async-start(bf16[32,4,16,128]{3,1,2,0:T(4,128)(2,1)} %broadcast_in_dim.104), calls=%async_computation | async-start | bytes 1048576 | tf_op jit(solution)/shard_map/all_to_all | solution.py:16
  33.0 1.6 copy-start.3
  35.8 6.2 %copy-start.9 = (s32[4]{0:T(128)S(1)}, s32[4]{0:T(128)}, u32[]{:S(2)}) copy-start(s32[4]{0:T(128)} %param.24) | copy-start | bytes 52
  35.9 6.2 %copy-start.5 = (bf16[4,16,128]{2,1,0:T(8,128)(2,1)S(1)}, bf16[4,16,128]{2,1,0:T(8,128)(2,1)}, u32[]{:S(2)}) copy-start(bf16[4,16,128]{2,1,0:T(8,128)(2,1)} %param.16) | copy-start | bytes 49156
  37.8 32.1 %all-to-all-start.1 = ((f32[128,2,8,130]{3,2,1,0:T(8,128)}), f32[128,2,8,130]{3,2,1,0:T(8,128)S(1)}, u32[]{:S(2)}, u32[]{:S(2)}) async-start(f32[128,2,8,130]{3,2,1,0:T(8,128)} %copy.135), calls=%async_computation.1 | async-start | bytes 4194304 | tf_op jit(solution)/shard_map/all_to_all | solution.py:34
  42.0 188.9 %all-reduce.3.cloned.1.call-start = ((), (), s32[]{:S(2)}) async-start(), calls=%async_computation.6 | async-start | bytes 7340032 | tf_op jit(solution)/shard_map/psum | solution.py:210
  77.2 1.0 copy-start.8
  77.8 27.9 %copy-start.4 = (bf16[128,256]{1,0:T(8,128)(2,1)S(1)}, bf16[128,256]{1,0:T(8,128)(2,1)}, u32[]{:S(2)}) copy-start(bf16[128,256]{1,0:T(8,128)(2,1)} %param.26) | copy-start | bytes 196612
  78.3 39.8 %copy-start.6 = (f32[256]{0:T(256)S(1)}, f32[256]{0:T(256)}, u32[]{:S(2)}) copy-start(f32[256]{0:T(256)} %param.27) | copy-start | bytes 3076
  118.0 4.2 %copy-start.1 = (bf16[256,7168]{1,0:T(8,128)(2,1)S(1)}, bf16[256,7168]{1,0:T(8,128)(2,1)}, u32[]{:S(2)}) copy-start(bf16[256,7168]{1,0:T(8,128)(2,1)} %param.29) | copy-start | bytes 11010052
  235.8 8.5 %all-to-all-start.5 = ((bf16[4,32,256]{2,1,0:T(8,128)(2,1)}), bf16[4,32,256]{2,1,0:T(8,128)(2,1)S(1)}, u32[]{:S(2)}, u32[]{:S(2)}) async-start(bf16[4,32,256]{2,1,0:T(8,128)(2,1)} %bitcast.30), calls=%async_computation.5 | async-start | bytes 131072 | tf_op jit(solution)/shard_map/all_to_all | solution.py:63
Sparse Core Ops, SparseCore 0:
  124.4 106.4 all-reduce.2
where the time goes:
time: 254 us; the launch traced here: 252 us
  waiting for transfers between devices  146 us (57%)
  blocking collectives  38.6 us (15%)
  matrix products  17.9 us (7%)
  starting transfers between devices  17.6 us (7%)
  local copies, waits for them, and re-layouts  13.8 us (5%)
  between operations  13.7 us (5%)
  other arithmetic  4.22 us (2%)
    psum x1, waiting for transfers between devices, on_device(): lax.psum(jnp.dot(normed, up_weight, preferred_element_type=jnp.float32).a...  107 us
    all_to_all x3, blocking collectives, copy_for_each(): return lax.all_to_all(copies, axis, split_axis=0, concat_axis=0, tiled=True)  38.6 us
    all_to_all x1, waiting for transfers between devices, sent_together(): lax.all_to_all(both, axis, split_axis=split_dim, concat_axis=concat_dim,...  26.3 us
    all_to_all x1, starting transfers between devices, copy_for_each(): return lax.all_to_all(copies, axis, split_axis=0, concat_axis=0, tiled=True)  9.43 us
    all_to_all x1, waiting for transfers between devices, copy_for_each(): return lax.all_to_all(copies, axis, split_axis=0, concat_axis=0, tiled=True)  8.56 us
    slice x4, local copies, waits for them, and re-layouts, sent_together(): piece = result[..., at:at + column.shape[along]]  7.57 us
  transfers between devices with their start and end apart: 4, of which 4 were waited for; matrix products, arithmetic and copies ran while one was open for 2% of the time, Pallas kernels for 0%

commit v1 on v0

v1 whole, which is shorter than its diff:
```python
import jax
import jax.numpy as jnp
from jax import lax
from jax.sharding import Mesh
from jax.sharding import PartitionSpec as P

D = 8192
CAP = 8
masked_score = -1e30
norm_eps = 1e-05
bf16 = jnp.bfloat16
f32 = jnp.float32
PLANE = ("z", "x")
NODE = ("z", "x", "core")
SWAP = [(0, 1), (1, 0)]


def exchange(x, axes):
    return lax.all_to_all(x, axes, split_axis=0, concat_axis=0, tiled=True)


def swapped(x):
    return lax.ppermute(x, "core", SWAP)


def rounded(x):
    return lax.reduce_precision(x, 8, 7)


def in_pieces(x):
    first = rounded(x)
    second = rounded(x - first)
    third = x - first - second
    return first.astype(bf16), second.astype(bf16), third.astype(bf16)


def attend(queries, keys, values, usable, scaling):
    scores = jnp.einsum("...qd,...ld->...ql", queries, keys, preferred_element_type=f32) * scaling
    scores = jnp.where(usable, scores, masked_score)
    highest = jnp.max(scores, axis=-1, keepdims=True)
    weights = jnp.where(usable, jnp.exp(scores - highest), 0.0)
    weighted = jnp.einsum(
        "...ql,...ld->...qd", weights.astype(bf16), values, preferred_element_type=f32
    )
    return highest, jnp.sum(weights, axis=-1, keepdims=True), weighted


def on_device(
    queries,
    root_keys,
    root_values,
    mid_keys,
    mid_values,
    leaf_keys,
    leaf_values,
    mid_length,
    leaf_length,
    branch_mid,
    residual,
    norm_gain,
    out_weight,
    gate_weight,
    up_weight,
    down_weight,
):
    core = lax.axis_index("core")
    other = 1 - core
    chip = lax.axis_index(PLANE)
    head_size = queries.shape[2]
    group = queries.shape[1] // 2
    scaling = head_size ** (-0.5)
    chips = 16

    halves = queries.reshape(4, 2, group, head_size).transpose(1, 0, 2, 3)
    sent = jnp.broadcast_to(halves[None], (chips, *halves.shape)).reshape(32, 4, group, head_size)
    gathered = exchange(sent, NODE).reshape(128, group, head_size)

    caches = (root_keys, root_values, mid_keys, mid_values, leaf_keys, leaf_values)

    def of_head(x, head):
        return lax.dynamic_index_in_dim(x, head, x.ndim - 2, keepdims=False).reshape(-1, head_size)

    kept = jnp.concatenate([of_head(x, core) for x in caches])
    arrived = swapped(jnp.concatenate([of_head(x, other) for x in caches]))
    spans, at = [], 0
    for x in caches:
        rows = x.size // 2 // head_size
        spans.append((at, at + rows))
        at += rows
    pair = [(kept[a:b], arrived[a:b]) for a, b in spans]
    lengths = (leaf_length, swapped(leaf_length))

    def ordered(a, b):
        return jnp.where(core == 0, jnp.stack([a, b]), jnp.stack([b, a]))

    hidden = gate_weight.shape[1] // 2

    def columns(w, half):
        return lax.dynamic_slice_in_dim(w, half * hidden, hidden, 1)

    def rows_of(w, half):
        return lax.dynamic_slice_in_dim(w, half * hidden, hidden, 0)

    gate_far = swapped(columns(gate_weight, other))
    up_far = swapped(columns(up_weight, other))
    down_far = swapped(rows_of(down_weight, other))
    gain_far = swapped(norm_gain)

    flat = gathered.reshape(128 * group, head_size)
    root_high, root_total, root_weighted = attend(
        flat, jnp.concatenate(pair[0]), jnp.concatenate(pair[1]), True, scaling
    )
    nodes = jnp.stack([2 * chip + core, 2 * chip + other])
    routing = branch_mid[:, 0]
    place = jnp.arange(128)
    earlier = (routing[None, :] == routing[:, None]) & (place[None, :] < place[:, None])
    rank = jnp.sum(earlier.astype(jnp.int32), axis=1)
    chosen = (routing[None, None, :] == nodes[:, None, None]) & (
        rank[None, None, :] == jnp.arange(CAP)[None, :, None]
    )
    picked = jnp.einsum(
        "ncb,bgd->ncgd", chosen.astype(bf16), gathered, preferred_element_type=f32
    ).astype(bf16)
    usable = jnp.arange(mid_keys.shape[1])[None, None, :] < mid_length[nodes][:, None, None]
    mid_high, mid_total, mid_weighted = attend(
        picked.reshape(2, CAP * group, head_size),
        jnp.stack(pair[2]),
        jnp.stack(pair[3]),
        usable,
        scaling,
    )
    exact = lax.Precision.HIGHEST
    spread = chosen.astype(f32)
    mid_all = jnp.concatenate([mid_weighted, mid_high, mid_total], axis=-1).reshape(2, CAP, group, -1)
    back = jnp.einsum("ncb,ncgd->bgd", spread, mid_all, precision=exact).reshape(128 * group, -1)
    covered = jnp.sum(spread, axis=(0, 1))
    lack = jnp.repeat((1.0 - covered) * masked_score, group)[:, None]
    back_weighted = back[:, :head_size]
    back_high = back[:, head_size : head_size + 1] + lack
    back_total = back[:, head_size + 1 :]
    high = jnp.maximum(root_high, back_high)
    root_factor = jnp.exp(root_high - high)
    back_factor = jnp.exp(back_high - high)
    total = root_total * root_factor + back_total * back_factor
    mean = (root_weighted * root_factor + back_weighted * back_factor) / total
    level = (high + jnp.log(total)).reshape(chips, -1)
    first, second, third = in_pieces(level)
    stats = jnp.stack(
        [
            jnp.concatenate([first, second], axis=1),
            jnp.concatenate([third, jnp.zeros_like(third)], axis=1),
        ],
        axis=1,
    )
    payload = jnp.concatenate([mean.astype(bf16).reshape(chips, 64, head_size), stats], axis=1)
    parts = exchange(payload, PLANE)
    means = parts[:, :64].astype(f32)
    stats = parts[:, 64:].astype(f32)
    level = stats[:, 0, :64] + stats[:, 0, 64:] + stats[:, 1, :64]
    mine = ordered(halves_of(queries, core, group), swapped(halves_of(queries, other, group)))
    leaf_usable = (
        jnp.arange(leaf_keys.shape[1])[None, None, :]
        < ordered(*lengths).reshape(8)[:, None, None]
    )
    leaf_high, leaf_total, leaf_weighted = attend(
        mine.reshape(8, group, head_size),
        ordered(*pair[4]).reshape(8, -1, head_size),
        ordered(*pair[5]).reshape(8, -1, head_size),
        leaf_usable,
        scaling,
    )
    leaf_high = leaf_high.reshape(64)
    high = jnp.maximum(jnp.max(level, axis=0), leaf_high)
    factor = jnp.exp(level - high[None])
    leaf_factor = jnp.exp(leaf_high - high)
    total = jnp.sum(factor, axis=0) + leaf_factor * leaf_total.reshape(64)
    weighted = jnp.sum(means * factor[:, :, None], axis=0) + leaf_factor[:, None] * leaf_weighted.reshape(64, head_size)
    attended = (weighted / total[:, None]).astype(bf16).reshape(8, group * head_size)

    near = exchange(jnp.broadcast_to(attended[None], (chips, *attended.shape)), PLANE)
    near = near.reshape(128, group * head_size)
    far = swapped(near)
    half_rows = out_weight.shape[0] // 2
    projected = jnp.dot(
        near, lax.dynamic_slice_in_dim(out_weight, core * half_rows, half_rows, 0), preferred_element_type=f32
    ) + jnp.dot(
        far, lax.dynamic_slice_in_dim(out_weight, other * half_rows, half_rows, 0), preferred_element_type=f32
    )
    shares = exchange(jnp.broadcast_to(projected.astype(bf16)[None], (4, *projected.shape)), "mp")
    stream = residual.astype(f32) + jnp.sum(shares.astype(f32), axis=0)
    stream_far = swapped(stream)
    squares = jnp.sum(stream * stream, axis=1) + jnp.sum(stream_far * stream_far, axis=1)
    scaled = (stream * norm_gain[None]).astype(bf16)
    scaled_far = (stream_far * gain_far[None]).astype(bf16)

    def both(w, far):
        return (
            jnp.dot(scaled, columns(w, core), preferred_element_type=f32)
            + jnp.dot(scaled_far, far, preferred_element_type=f32)
        ).astype(bf16)

    pieces = jnp.stack(in_pieces(squares), axis=1)
    pieces = jnp.pad(pieces, ((0, 0), (0, 125)))
    payload = jnp.concatenate([both(gate_weight, gate_far), both(up_weight, up_far), pieces], axis=1)
    parts = exchange(payload.reshape(chips, 8, -1), PLANE)
    summed = jnp.sum(parts.astype(f32), axis=0)
    inverse = lax.rsqrt(jnp.sum(summed[:, 2 * hidden : 2 * hidden + 3], axis=1, keepdims=True) / D + norm_eps)
    gate = summed[:, :hidden] * inverse
    upward = summed[:, hidden : 2 * hidden] * inverse
    act = (jax.nn.silu(gate) * upward).astype(bf16)
    acts = exchange(jnp.broadcast_to(act[None], (chips, *act.shape)), PLANE).reshape(128, hidden)
    own = jnp.dot(acts, rows_of(down_weight, core), preferred_element_type=f32).astype(bf16)
    partner = jnp.dot(acts, down_far, preferred_element_type=f32).astype(bf16)
    blocks = ordered(own, partner).reshape(8, 32, -1)
    arrived = exchange(blocks, ("core", "mp"))
    rows = lax.dynamic_slice_in_dim(stream, lax.axis_index("mp") * 32, 32, 0)
    return (rows + jnp.sum(arrived.astype(f32), axis=0)).astype(bf16)


def halves_of(queries, half, group):
    return lax.dynamic_slice_in_dim(queries, half * group, group, 1)


def solution(mesh):
    fine = Mesh(mesh.devices.reshape(4, 4, 2, 4), ("z", "x", "core", "mp"))
    in_specs = (
        P(NODE, "mp", None),
        P(NODE, "mp", None),
        P(NODE, "mp", None),
        P(NODE, None, "mp", None),
        P(NODE, None, "mp", None),
        P(NODE, None, "mp", None),
        P(NODE, None, "mp", None),
        P(),
        P(NODE),
        P(),
        P(None, NODE),
        P(NODE),
        P("mp", NODE),
        P(NODE, "mp"),
        P(NODE, "mp"),
        P("mp", NODE),
    )
    return jax.shard_map(
        on_device, mesh=fine, in_specs=in_specs, out_specs=P("mp", NODE), check_vma=False
    )
```

time: 254 us -> 170 us (0.67)
  waiting for transfers between devices: 146 us -> 51.6 us
  local copies, waits for them, and re-layouts: 13.8 us -> 37 us
  blocking collectives: 38.6 us -> 17.6 us
  starting transfers between devices: 17.6 us -> 37.3 us
  between operations: 13.7 us -> 0.6 us
  other arithmetic: 4.22 us -> 7.33 us
    psum x1 -> x0, waiting for transfers between devices: 107 us -> none  [on_device(): lax.psum(jnp.dot(normed, up_weight, preferred_element_type=jnp.float32).a...]
    all_to_all x3 -> x1, blocking collectives: 38.6 us -> 17.6 us  [exchange(): return lax.all_to_all(x, axes, split_axis=0, concat_axis=0, tiled=True)]
    dynamic_slice x1 -> x6, local copies, waits for them, and re-layouts: 1.24 us -> 17 us  [the longest x3 8.35 us: of_head(): lax.dynamic_index_in_dim(x, head, x.ndim - 2, keepdims=False)]
    all_to_all x3 -> x6, waiting for transfers between devices: 39.3 us -> 51.6 us  [exchange(): return lax.all_to_all(x, axes, split_axis=0, concat_axis=0, tiled=True)]
    all_to_all x3 -> x6, starting transfers between devices: 17.5 us -> 29.8 us  [exchange(): return lax.all_to_all(x, axes, split_axis=0, concat_axis=0, tiled=True)]
    unnamed x22 -> x65, local copies, waits for them, and re-layouts: 1 us -> 10.6 us
    ppermute x0 -> x9, starting transfers between devices: none -> 7.58 us  [swapped(): return lax.ppermute(x, 'core', SWAP)]
    slice x4 -> x2, local copies, waits for them, and re-layouts: 7.57 us -> 1.2 us  [the longest x1 1 us: on_device(): pair = [(kept[a:b], arrived[a:b]) for a, b in spans]]
  transfers between devices with their start and end apart: 4 -> 15, of which waited for: 4 -> 6; matrix products, arithmetic and copies ran while one was open for 2% -> 15% of each run, Pallas kernels for 0% -> 0%
where the time goes in v1:
time: 170 us; the launch traced here: 169 us
  waiting for transfers between devices  51.6 us (30%)
  starting transfers between devices  37.3 us (22%)
  local copies, waits for them, and re-layouts  37 us (22%)
  matrix products  17.6 us (10%)
  blocking collectives  17.6 us (10%)
  other arithmetic  7.33 us (4%)
    all_to_all x6, waiting for transfers between devices, exchange(): return lax.all_to_all(x, axes, split_axis=0, concat_axis=0, tiled=True)  51.6 us
    all_to_all x6, starting transfers between devices, exchange(): return lax.all_to_all(x, axes, split_axis=0, concat_axis=0, tiled=True)  29.8 us
    all_to_all x1, blocking collectives, exchange(): return lax.all_to_all(x, axes, split_axis=0, concat_axis=0, tiled=True)  17.6 us
    unnamed x65, local copies, waits for them, and re-layouts  10.6 us
    dynamic_slice x3, local copies, waits for them, and re-layouts, of_head(): lax.dynamic_index_in_dim(x, head, x.ndim - 2, keepdims=False)  8.35 us
    ppermute x9, starting transfers between devices, swapped(): return lax.ppermute(x, 'core', SWAP)  7.58 us
    dynamic_slice x2, local copies, waits for them, and re-layouts, columns(): return lax.dynamic_slice_in_dim(w, half * hidden, hidden, 1)  5.8 us
    dot_general x2, matrix products, both(): jnp.dot(scaled_far, far, preferred_element_type=f32)  4.4 us
  transfers between devices with their start and end apart: 15, of which 6 were waited for; matrix products, arithmetic and copies ran while one was open for 15% of the time, Pallas kernels for 0%

profile of v1, /device:TPU:1, one launch (start us, length us, event | category | flops | bytes accessed | tf_op | source)
XLA Modules:
  0.0 169.1 jit_solution(17925212889174794411)
XLA Ops:
  0.0 3.2 %constant_dynamic-slice_fusion.8 = (bf16[512,1,128]{2,1,0:T(2,128)(2,1)}, bf16[512,1,128]{2,1,0:T(2,128)(2,1)S(1)}, bf16[512,1,128]{2,1,0:T(2,128)(2,1)S(1)}, bf16[512,1,128]{2,1,0:T(2,128)(2,1)}) fusion(bf16[512,2,128]{2,1,0:T(2,128)(2,1)} %param.18, s32[]{:T(128)S(6)} %select_n.133, s32[]{:T(128)S(6)} %select_n.134, bf16[512,2,128]{2,1,0:T(2,128)(2,1)} %param.17), kind=kLoop, calls=%fused_computation.152 | loop fusion | bytes 1048584 | tf_op jit(solution)/shard_map/jit(dynamic_index_in_dim)/dynamic_slice | solution.py:81
  3.2 0.7 fusion.72
  3.9 2.2 %constant_dynamic-slice_fusion.3 = (bf16[4,256,1,128]{3,2,1,0:T(2,128)(2,1)S(1)}, bf16[4,256,1,128]{3,2,1,0:T(2,128)(2,1)S(1)}, bf16[4,256,1,128]{3,2,1,0:T(2,128)(2,1)S(1)}, bf16[4,256,1,128]{3,2,1,0:T(2,128)(2,1)S(1)}) fusion(bf16[4,256,2,128]{3,2,1,0:T(2,128)(2,1)S(1)} %copy-done.5, s32[]{:T(128)S(6)} %select_n.133, s32[]{:T(128)S(6)} %select_n.134, ...), kind=kLoop, calls=%fused_computation.147 | loop fusion | bytes 2097160 | tf_op jit(solution)/shard_map/jit(dynamic_index_in_dim)/dynamic_slice | solution.py:81
  6.2 0.7 fusion.71
  6.9 0.3 copy-done.7
  7.3 3.0 %constant_dynamic-slice_fusion.6 = (bf16[1,1024,1,128]{3,2,1,0:T(2,128)(2,1)S(1)}, bf16[1,1024,1,128]{3,2,1,0:T(2,128)(2,1)S(1)}, bf16[1,1024,1,128]{3,2,1,0:T(2,128)(2,1)S(1)}, bf16[1,1024,1,128]{3,2,1,0:T(2,128)(2,1)}) fusion(bf16[1,1024,2,128]{3,2,1,0:T(2,128)(2,1)S(1)} %copy-done.7, s32[]{:T(128)S(6)} %select_n.133, s32[]{:T(128)S(6)} %select_n.134, ...), kind=kLoop, calls=%fused_computation.150 | loop fusion | bytes 2097160 | tf_op jit(solution)/shard_map/jit(dynamic_index_in_dim)/dynamic_slice | solution.py:81
  10.3 0.7 fusion.62
  11.0 0.8 fusion.61
  11.8 0.7 constant_dynamic-update-slice_fusion.1
  12.5 0.7 constant_dynamic-update-slice_fusion
  13.2 1.4 collective-permute-start
  14.7 0.4 collective-permute-start.1
  15.2 0.8 broadcast_in_dim.53
  15.9 8.2 %all-to-all-start = ((bf16[32,4,8,128]{3,2,1,0:T(8,128)(2,1)}), bf16[32,4,8,128]{3,2,1,0:T(8,128)(2,1)S(1)}, u32[]{:S(2)}, u32[]{:S(2)}) async-start(bf16[32,4,8,128]{3,2,1,0:T(8,128)(2,1)} %bitcast.9), calls=%async_computation | async-start | bytes 524288 | tf_op jit(solution)/shard_map/all_to_all | solution.py:19
  24.1 0.7 copy.229
  24.9 1.0 copy.258
  25.8 1.1 copy.256
  27.4 0.7 broadcast_in_dim_reshape.2
  28.1 0.7 copy.257
  28.8 0.7 copy.230
  29.6 0.6 gather_fusion
  30.5 0.7 iota_compare_fusion.2
  31.1 1.8 %all-to-all-done = bf16[32,4,8,128]{3,2,1,0:T(8,128)(2,1)S(1)} async-done(((bf16[32,4,8,128]{3,2,1,0:T(8,128)(2,1)}), bf16[32,4,8,128]{3,2,1,0:T(8,128)(2,1)S(1)}, u32[]{:S(2)}, u32[]{:S(2)}) %all-to-all-start) | async-done | bytes 262176 | tf_op jit(solution)/shard_map/all_to_all | solution.py:19
  33.3 2.1 %slice_bitcast_fusion = (bf16[1,1024,128]{2,1,0:T(8,128)(2,1)}, bf16[1,1024,128]{2,1,0:T(8,128)(2,1)}, bf16[1,1024,128]{2,1,0:T(8,128)(2,1)S(1)}, bf16[1,1024,128]{2,1,0:T(8,128)(2,1)S(1)}) fusion(bf16[5120,128]{1,0:T(8,128)(2,1)} %collective-permute-done), kind=kLoop, calls=%fused_computation.62 | loop fusion | bytes 2097152 | tf_op jit(solution)/shard_map/stack | solution.py:94
  35.3 0.4 fusion.115
  36.0 0.3 convolution_bitcast_fusion.1
  36.8 1.4 convolution_bitcast_fusion
  38.2 0.5 copy.204
  38.8 0.8 copy.227
  39.8 1.0 fusion.113
  40.8 0.7 multiply_reduce_fusion
  41.6 0.7 fusion.3
  42.3 1.2 copy-done.2
  43.8 3.4 %fusion.31 = bf16[1024,128]{1,0:T(8,128)(2,1)S(1)} fusion(f32[1024,1024]{1,0:T(8,128)} %copy-done.2, f32[1024]{0:T(1024)S(1)} %get-tuple-element.49, f32[1024,130]{1,0:T(8,128)S(1)} %bitcast.134, bf16[512,128]{1,0:T(8,128)(2,1)S(1)} %get-tuple-element.23, bf16[512,128]{1,0:T(8,128)(2,1)S(1)} %bitcast.148, f32[1024]{0:T(1024)S(1)} %bitcast.156, ...), kind=kOutput, calls=%fused_computation.33 | convolution fusion | flops 272760832 | bytes 5259264 | tf_op jit(solution)/shard_map/...ql,...ld->...qd/dot_general | solution.py:42
  47.2 0.7 pad_maximum_fusion
  47.9 4.9 %all-to-all-start.1 = ((bf16[16,66,128]{2,1,0:T(8,128)(2,1)}), bf16[16,66,128]{2,1,0:T(8,128)(2,1)S(1)}, u32[]{:S(2)}, u32[]{:S(2)}) async-start(bf16[16,66,128]{2,1,0:T(8,128)(2,1)} %pad_maximum_fusion), calls=%async_computation.1 | async-start | bytes 589824 | tf_op jit(solution)/shard_map/all_to_all | solution.py:19
  52.9 0.3 fusion.116
  53.6 7.7 %all-to-all-done.1 = bf16[16,66,128]{2,1,0:T(8,128)(2,1)S(1)} async-done(((bf16[16,66,128]{2,1,0:T(8,128)(2,1)}), bf16[16,66,128]{2,1,0:T(8,128)(2,1)S(1)}, u32[]{:S(2)}, u32[]{:S(2)}) %all-to-all-start.1) | async-done | bytes 270368 | tf_op jit(solution)/shard_map/all_to_all | solution.py:19
  62.2 0.7 broadcast_in_dim.101
  63.0 3.5 %all-to-all-start.2 = ((bf16[16,8,1024]{2,1,0:T(8,128)(2,1)}), bf16[16,8,1024]{2,1,0:T(8,128)(2,1)S(1)}, u32[]{:S(2)}, u32[]{:S(2)}) async-start(bf16[16,8,1024]{2,1,0:T(8,128)(2,1)} %broadcast_in_dim.101), calls=%async_computation.2 | async-start | bytes 524288 | tf_op jit(solution)/shard_map/all_to_all | solution.py:19
  66.5 7.5 %all-to-all-done.2 = bf16[16,8,1024]{2,1,0:T(8,128)(2,1)S(1)} async-done(((bf16[16,8,1024]{2,1,0:T(8,128)(2,1)}), bf16[16,8,1024]{2,1,0:T(8,128)(2,1)S(1)}, u32[]{:S(2)}, u32[]{:S(2)}) %all-to-all-start.2) | async-done | bytes 262176 | tf_op jit(solution)/shard_map/all_to_all | solution.py:19
  74.0 2.7 %collective-permute-start.3 = (bf16[128,1024]{1,0:T(8,128)(2,1)S(1)}, bf16[128,1024]{1,0:T(8,128)(2,1)S(1)}, u32[]{:S(2)}, u32[]{:S(2)}) collective-permute-start(bf16[128,1024]{1,0:T(8,128)(2,1)S(1)} %bitcast.138), channel_id=1, source_target_pairs={{0,4},{4,0},{1,5},{5,1},{2,6},{6,2},{3,7},{7,3},{8,12},{12,8},{9,1... | collective-permute-start | bytes 786440 | tf_op jit(solution)/shard_map/ppermute | solution.py:23
  76.7 2.9 %constant_dynamic-slice_fusion.2 = bf16[256,3584]{1,0:T(8,128)(2,1)} fusion(bf16[256,7168]{1,0:T(8,128)(2,1)} %param.29, s32[]{:T(128)S(6)} %select_n.158), kind=kLoop, calls=%fused_computation.143 | loop fusion | bytes 3670020 | tf_op jit(solution)/shard_map/dynamic_slice | solution.py:99
  80.1 0.7 broadcast_in_dim.102
  80.8 4.2 %all-to-all-start.3 = ((bf16[4,128,256]{2,1,0:T(8,128)(2,1)}), bf16[4,128,256]{2,1,0:T(8,128)(2,1)S(1)}, u32[]{:S(2)}, u32[]{:S(2)}) async-start(bf16[4,128,256]{2,1,0:T(8,128)(2,1)} %broadcast_in_dim.102), calls=%async_computation.3 | async-start | bytes 524288 | tf_op jit(solution)/shard_map/all_to_all | solution.py:19
  85.0 2.9 %constant_dynamic-slice_fusion.1 = bf16[256,3584]{1,0:T(8,128)(2,1)} fusion(bf16[256,7168]{1,0:T(8,128)(2,1)} %param.30, s32[]{:T(128)S(6)} %select_n.158), kind=kLoop, calls=%fused_computation.141 | loop fusion | bytes 3670020 | tf_op jit(solution)/shard_map/dynamic_slice | solution.py:99
  87.9 0.8 collective-permute-start.7
  88.7 2.0 %all-to-all-done.3 = bf16[4,128,256]{2,1,0:T(8,128)(2,1)S(1)} async-done(((bf16[4,128,256]{2,1,0:T(8,128)(2,1)}), bf16[4,128,256]{2,1,0:T(8,128)(2,1)S(1)}, u32[]{:S(2)}, u32[]{:S(2)}) %all-to-all-start.3) | async-done | bytes 262176 | tf_op jit(solution)/shard_map/all_to_all | solution.py:19
  90.8 2.0 %collective-permute-start.4 = (f32[128,256]{1,0:T(8,128)S(1)}, f32[128,256]{1,0:T(8,128)S(1)}, u32[]{:S(2)}, u32[]{:S(2)}) collective-permute-start(f32[128,256]{1,0:T(8,128)S(1)} %get-tuple-element.6), channel_id=1, source_target_pairs={{0,4},{4,0},{1,5},{5,1},{2,6},{6,2},{3,7},{7,3},{8,12},{12,8},{9,1... | collective-permute-start | bytes 393224 | tf_op jit(solution)/shard_map/ppermute | solution.py:23
  92.8 3.2 %fusion.15 = f32[128,3584]{1,0:T(8,128)} fusion(bf16[256,7168]{1,0:T(8,128)(2,1)} %param.29, s32[]{:T(128)S(6)} %select_n.157, f32[128,256]{1,0:T(8,128)S(1)} %get-tuple-element.6, f32[256]{0:T(256)S(1)} %copy-done.22), kind=kOutput, calls=%fused_computation.21 | convolution fusion | flops 234946560 | bytes 3802116 | tf_op jit(solution)/shard_map/dot_general | solution.py:198
  96.0 0.4 fusion.13
  96.8 2.5 %fusion = bf16[128,3584]{1,0:T(8,128)(2,1)S(1)} fusion(f32[128,3584]{1,0:T(8,128)} %fusion.15, bf16[256,3584]{1,0:T(8,128)(2,1)} %collective-permute-done.6, f32[128,256]{1,0:T(8,128)S(1)} %collective-permute-done.4, f32[256]{0:T(256)S(1)} %collective-permute-done.5), kind=kOutput, calls=%fused_computation.3 | convolution fusion | flops 235864064 | bytes 4719616 | tf_op jit(solution)/shard_map/dot_general | solution.py:199
  99.3 1.9 %fusion.1 = bf16[128,3584]{1,0:T(8,128)(2,1)S(1)} fusion(f32[128,3584]{1,0:T(8,128)S(1)} %fusion.13, bf16[256,3584]{1,0:T(8,128)(2,1)} %collective-permute-done.7, f32[128,256]{1,0:T(8,128)S(1)} %collective-permute-done.4, f32[256]{0:T(256)S(1)} %collective-permute-done.5), kind=kOutput, calls=%fused_computation.4 | convolution fusion | flops 235864064 | bytes 4719616 | tf_op jit(solution)/shard_map/dot_general | solution.py:199
  101.2 1.4 fusion.10
  102.6 3.7 %all-to-all-start.4 = ((bf16[16,8,7296]{2,1,0:T(8,128)(2,1)}), bf16[16,8,7296]{2,1,0:T(8,128)(2,1)S(1)}, u32[]{:S(2)}, u32[]{:S(2)}) async-start(bf16[16,8,7296]{2,1,0:T(8,128)(2,1)} %fusion.10), calls=%async_computation.4 | async-start | bytes 3735552 | tf_op jit(solution)/shard_map/all_to_all | solution.py:19
  106.3 2.9 %constant_dynamic-slice_fusion = bf16[3584,256]{1,0:T(8,128)(2,1)} fusion(bf16[7168,256]{1,0:T(8,128)(2,1)} %param.31, s32[]{:T(128)S(6)} %select_n.158), kind=kLoop, calls=%fused_computation.139 | loop fusion | bytes 3670020 | tf_op jit(solution)/shard_map/dynamic_slice | solution.py:102
  109.3 27.4 %all-to-all-done.4 = bf16[16,8,7296]{2,1,0:T(8,128)(2,1)S(1)} async-done(((bf16[16,8,7296]{2,1,0:T(8,128)(2,1)}), bf16[16,8,7296]{2,1,0:T(8,128)(2,1)S(1)}, u32[]{:S(2)}, u32[]{:S(2)}) %all-to-all-start.4) | async-done | bytes 1867808 | tf_op jit(solution)/shard_map/all_to_all | solution.py:19
  137.4 17.6 %all_to_all.35 = bf16[16,8,3584]{2,1,0:T(8,128)(2,1)S(1)} all-to-all(bf16[16,8,3584]{2,1,0:T(8,128)(2,1)S(1)} %broadcast_in_dim.103), channel_id=1, replica_groups=mesh['z'=4,'x'=4,'core'=2,'mp'=4] {'z','x'}, dimensions={0} | all-to-all | bytes 1835008 | tf_op jit(solution)/shard_map/all_to_all | solution.py:19
  155.0 0.4 fusion.35
  155.4 1.9 %fusion.34 = bf16[1,128,256]{2,1,0:T(8,128)(2,1)S(1)} fusion(bf16[3584,256]{1,0:T(8,128)(2,1)} %collective-permute-done.8, bf16[16,8,3584]{2,1,0:T(8,128)(2,1)S(1)} %all_to_all.35), kind=kOutput, calls=%fused_computation.34 | convolution fusion | flops 234913792 | bytes 2818048 | tf_op jit(solution)/shard_map/dot_general | solution.py:213
  157.3 0.7 maximum_select_fusion.2
  158.0 5.3 %all-to-all-start.6 = ((bf16[8,32,256]{2,1,0:T(8,128)(2,1)}), bf16[8,32,256]{2,1,0:T(8,128)(2,1)S(1)}, u32[]{:S(2)}, u32[]{:S(2)}) async-start(bf16[8,32,256]{2,1,0:T(8,128)(2,1)} %bitcast.58), calls=%async_computation.6 | async-start | bytes 262144 | tf_op jit(solution)/shard_map/all_to_all | solution.py:19
  163.3 5.2 %all-to-all-done.6 = bf16[8,32,256]{2,1,0:T(8,128)(2,1)S(1)} async-done(((bf16[8,32,256]{2,1,0:T(8,128)(2,1)}), bf16[8,32,256]{2,1,0:T(8,128)(2,1)S(1)}, u32[]{:S(2)}, u32[]{:S(2)}) %all-to-all-start.6) | async-done | bytes 131104 | tf_op jit(solution)/shard_map/all_to_all | solution.py:19
  168.5 0.6 add_convert_fusion
  (127 shorter events, 5.9 us)
Async XLA Ops:
  0.0 79.6 %copy-start = (bf16[2048,256]{1,0:T(8,128)(2,1)S(1)}, bf16[2048,256]{1,0:T(8,128)(2,1)}, u32[]{:S(2)}) copy-start(bf16[2048,256]{1,0:T(8,128)(2,1)} %param.28) | copy-start | bytes 3145732
  0.0 3.9 %copy-start.6 = (bf16[4,256,2,128]{3,2,1,0:T(2,128)(2,1)S(1)}, bf16[4,256,2,128]{3,2,1,0:T(2,128)(2,1)}, u32[]{:S(2)}) copy-start(bf16[4,256,2,128]{3,2,1,0:T(2,128)(2,1)} %param.21) | copy-start | bytes 1572868
  0.0 3.9 %copy-start.5 = (bf16[4,256,2,128]{3,2,1,0:T(2,128)(2,1)S(1)}, bf16[4,256,2,128]{3,2,1,0:T(2,128)(2,1)}, u32[]{:S(2)}) copy-start(bf16[4,256,2,128]{3,2,1,0:T(2,128)(2,1)} %param.22) | copy-start | bytes 1572868
  6.1 1.1 copy-start.7
  6.1 1.2 copy-start.8
  10.3 4.4 %copy-start.16 = (bf16[4,16,128]{2,1,0:T(8,128)(2,1)S(1)}, bf16[4,16,128]{2,1,0:T(8,128)(2,1)}, u32[]{:S(2)}) copy-start(bf16[4,16,128]{2,1,0:T(8,128)(2,1)} %param.16) | copy-start | bytes 49156
  10.3 4.4 %copy-start.23 = (s32[4]{0:T(128)S(1)}, s32[4]{0:T(128)}, u32[]{:S(2)}) copy-start(s32[4]{0:T(128)} %param.24) | copy-start | bytes 52
  12.5 14.4 %copy-start.24 = (s32[128,1]{0,1:T(1,128)S(1)}, s32[128,1]{0,1:T(1,128)}, u32[]{:S(2)}) copy-start(s32[128,1]{0,1:T(1,128)} %param.25) | copy-start | bytes 1540
  13.2 20.0 %collective-permute-start = (bf16[5120,128]{1,0:T(8,128)(2,1)}, bf16[5120,128]{1,0:T(8,128)(2,1)}, u32[]{:S(2)}, u32[]{:S(2)}) collective-permute-start(bf16[5120,128]{1,0:T(8,128)(2,1)} %constant_dynamic-update-slice_fusion), channel_id=1, source_target_pairs={{0,4},{4,0},{1,5},{5,1},{2,6},{6,2},{3,7},{7,3},{8,12},{12,8},{9,1... | collective-permute-start | bytes 3932168 | tf_op jit(solution)/shard_map/ppermute | solution.py:23
  14.6 16.5 %collective-permute-start.2 = (bf16[4,8,128]{2,1,0:T(8,128)(2,1)S(1)}, bf16[4,8,128]{2,1,0:T(8,128)(2,1)S(1)}, u32[]{:S(2)}, u32[]{:S(2)}) collective-permute-start(bf16[4,8,128]{2,1,0:T(8,128)(2,1)S(1)} %get-tuple-element.40), channel_id=1, source_target_pairs={{0,4},{4,0},{1,5},{5,1},{2,6},{6,2},{3,7},{7,3},{8,12},{12,8},{9,1... | collective-permute-start | bytes 24584 | tf_op jit(solution)/shard_map/ppermute | solution.py:23
  14.7 15.6 %collective-permute-start.1 = (s32[4]{0:T(128)S(1)}, s32[4]{0:T(128)S(1)}, u32[]{:S(2)}, u32[]{:S(2)}) collective-permute-start(s32[4]{0:T(128)S(1)} %copy-done.23), channel_id=1, source_target_pairs={{0,4},{4,0},{1,5},{5,1},{2,6},{6,2},{3,7},{7,3},{8,12},{12,8},{9,1... | collective-permute-start | bytes 56 | tf_op jit(solution)/shard_map/ppermute | solution.py:23
  15.2 13.0 %copy-start.11 = (bf16[512,1,128]{2,1,0:T(2,128)(2,1)S(1)}, bf16[512,1,128]{2,1,0:T(2,128)(2,1)}, u32[]{:S(2)}) copy-start(bf16[512,1,128]{2,1,0:T(2,128)(2,1)} %get-tuple-element.35) | copy-start | bytes 393220
  15.9 17.1 %all-to-all-start = ((bf16[32,4,8,128]{3,2,1,0:T(8,128)(2,1)}), bf16[32,4,8,128]{3,2,1,0:T(8,128)(2,1)S(1)}, u32[]{:S(2)}, u32[]{:S(2)}) async-start(bf16[32,4,8,128]{3,2,1,0:T(8,128)(2,1)} %bitcast.9), calls=%async_computation | async-start | bytes 524288 | tf_op jit(solution)/shard_map/all_to_all | solution.py:19
  24.8 4.8 %copy-start.1 = (s32[32]{0:T(128)S(1)}, s32[32]{0:T(128)}, u32[]{:S(2)}) copy-start(s32[32]{0:T(128)} %param.23) | copy-start | bytes 388
  27.3 6.0 %copy-start.21 = (pred[2,128]{1,0:T(4,128)(4,1)}, pred[2,128]{1,0:T(4,128)(4,1)S(1)}, u32[]{:S(2)}) copy-start(pred[2,128]{1,0:T(4,128)(4,1)S(1)} %broadcast_compare_fusion) | copy-start | bytes 772
  27.3 6.0 %copy-start.20 = (pred[8,128]{1,0:T(8,128)(4,1)}, pred[8,128]{1,0:T(8,128)(4,1)S(1)}, u32[]{:S(2)}) copy-start(pred[8,128]{1,0:T(8,128)(4,1)S(1)} %iota_compare_fusion.4) | copy-start | bytes 3076
  41.5 2.0 %copy-start.2 = (f32[1024,1024]{1,0:T(8,128)}, f32[1024,1024]{1,0:T(8,128)S(1)}, u32[]{:S(2)}) copy-start(f32[1024,1024]{1,0:T(8,128)S(1)} %get-tuple-element.50) | copy-start | bytes 12582916
  41.5 1.9 %copy-start.18 = (f32[1024,1]{0,1:T(1,128)S(1)}, f32[1024,1]{0,1:T(1,128)}, u32[]{:S(2)}) copy-start(f32[1024,1]{0,1:T(1,128)} %copy.227) | copy-start | bytes 12292
  41.6 1.9 %copy-start.19 = (f32[1024,1]{0,1:T(1,128)S(1)}, f32[1024,1]{0,1:T(1,128)}, u32[]{:S(2)}) copy-start(f32[1024,1]{0,1:T(1,128)} %broadcast_in_dim_reshape.2) | copy-start | bytes 12292
  41.6 2.2 %copy-start.14 = (bf16[512,1,128]{2,0,1:T(8,128)(2,1)S(1)}, bf16[512,1,128]{2,0,1:T(8,128)(2,1)}, u32[]{:S(2)}) copy-start(bf16[512,1,128]{2,0,1:T(8,128)(2,1)} %copy.257) | copy-start | bytes 393220
  43.8 9.0 %copy-start.9 = (bf16[4,256,1,128]{3,1,0,2:T(8,128)(2,1)S(1)}, bf16[4,256,1,128]{3,1,0,2:T(8,128)(2,1)}, u32[]{:S(2)}) copy-start(bf16[4,256,1,128]{3,1,0,2:T(8,128)(2,1)} %copy.229) | copy-start | bytes 786436
  43.8 9.0 %copy-start.13 = (bf16[1,1024,128]{2,1,0:T(8,128)(2,1)S(1)}, bf16[1,1024,128]{2,1,0:T(8,128)(2,1)}, u32[]{:S(2)}) copy-start(bf16[1,1024,128]{2,1,0:T(8,128)(2,1)} %get-tuple-element.20) | copy-start | bytes 786436
  47.1 5.8 %copy-start.17 = (pred[8,256]{1,0:T(8,128)(4,1)S(1)}, pred[8,256]{1,0:T(8,128)(4,1)}, u32[]{:S(2)}) copy-start(pred[8,256]{1,0:T(8,128)(4,1)} %iota_compare_fusion.2) | copy-start | bytes 6148
  47.1 6.3 %copy-start.10 = (bf16[4,256,1,128]{3,1,0,2:T(8,128)(2,1)S(1)}, bf16[4,256,1,128]{3,1,0,2:T(8,128)(2,1)}, u32[]{:S(2)}) copy-start(bf16[4,256,1,128]{3,1,0,2:T(8,128)(2,1)} %copy.230) | copy-start | bytes 786436
  47.2 6.3 %copy-start.12 = (bf16[1,1024,128]{2,1,0:T(8,128)(2,1)S(1)}, bf16[1,1024,128]{2,1,0:T(8,128)(2,1)}, u32[]{:S(2)}) copy-start(bf16[1,1024,128]{2,1,0:T(8,128)(2,1)} %get-tuple-element.19) | copy-start | bytes 786436
  47.9 13.3 %all-to-all-start.1 = ((bf16[16,66,128]{2,1,0:T(8,128)(2,1)}), bf16[16,66,128]{2,1,0:T(8,128)(2,1)S(1)}, u32[]{:S(2)}, u32[]{:S(2)}) async-start(bf16[16,66,128]{2,1,0:T(8,128)(2,1)} %pad_maximum_fusion), calls=%async_computation.1 | async-start | bytes 589824 | tf_op jit(solution)/shard_map/all_to_all | solution.py:19
  63.0 11.0 %all-to-all-start.2 = ((bf16[16,8,1024]{2,1,0:T(8,128)(2,1)}), bf16[16,8,1024]{2,1,0:T(8,128)(2,1)S(1)}, u32[]{:S(2)}, u32[]{:S(2)}) async-start(bf16[16,8,1024]{2,1,0:T(8,128)(2,1)} %broadcast_in_dim.101), calls=%async_computation.2 | async-start | bytes 524288 | tf_op jit(solution)/shard_map/all_to_all | solution.py:19
  74.0 5.8 %collective-permute-start.3 = (bf16[128,1024]{1,0:T(8,128)(2,1)S(1)}, bf16[128,1024]{1,0:T(8,128)(2,1)S(1)}, u32[]{:S(2)}, u32[]{:S(2)}) collective-permute-start(bf16[128,1024]{1,0:T(8,128)(2,1)S(1)} %bitcast.138), channel_id=1, source_target_pairs={{0,4},{4,0},{1,5},{5,1},{2,6},{6,2},{3,7},{7,3},{8,12},{12,8},{9,1... | collective-permute-start | bytes 786440 | tf_op jit(solution)/shard_map/ppermute | solution.py:23
  79.6 17.2 %collective-permute-start.6 = (bf16[256,3584]{1,0:T(8,128)(2,1)}, bf16[256,3584]{1,0:T(8,128)(2,1)}, u32[]{:S(2)}, u32[]{:S(2)}) collective-permute-start(bf16[256,3584]{1,0:T(8,128)(2,1)} %constant_dynamic-slice_fusion.2), channel_id=1, source_target_pairs={{0,4},{4,0},{1,5},{5,1},{2,6},{6,2},{3,7},{7,3},{8,12},{12,8},{9,1... | collective-permute-start | bytes 5505032 | tf_op jit(solution)/shard_map/ppermute | solution.py:23
  80.8 9.8 %all-to-all-start.3 = ((bf16[4,128,256]{2,1,0:T(8,128)(2,1)}), bf16[4,128,256]{2,1,0:T(8,128)(2,1)S(1)}, u32[]{:S(2)}, u32[]{:S(2)}) async-start(bf16[4,128,256]{2,1,0:T(8,128)(2,1)} %broadcast_in_dim.102), calls=%async_computation.3 | async-start | bytes 524288 | tf_op jit(solution)/shard_map/all_to_all | solution.py:19
  85.0 3.7 %copy-start.22 = (f32[256]{0:T(256)S(1)}, f32[256]{0:T(256)}, u32[]{:S(2)}) copy-start(f32[256]{0:T(256)} %param.27) | copy-start | bytes 3076
  85.0 5.7 %copy-start.15 = (bf16[128,256]{1,0:T(8,128)(2,1)S(1)}, bf16[128,256]{1,0:T(8,128)(2,1)}, u32[]{:S(2)}) copy-start(bf16[128,256]{1,0:T(8,128)(2,1)} %param.26) | copy-start | bytes 196612
  87.9 11.4 %collective-permute-start.7 = (bf16[256,3584]{1,0:T(8,128)(2,1)}, bf16[256,3584]{1,0:T(8,128)(2,1)}, u32[]{:S(2)}, u32[]{:S(2)}) collective-permute-start(bf16[256,3584]{1,0:T(8,128)(2,1)} %constant_dynamic-slice_fusion.1), channel_id=1, source_target_pairs={{0,4},{4,0},{1,5},{5,1},{2,6},{6,2},{3,7},{7,3},{8,12},{12,8},{9,1... | collective-permute-start | bytes 5505032 | tf_op jit(solution)/shard_map/ppermute | solution.py:23
  88.7 8.1 %collective-permute-start.5 = (f32[256]{0:T(256)S(1)}, f32[256]{0:T(256)S(1)}, u32[]{:S(2)}, u32[]{:S(2)}) collective-permute-start(f32[256]{0:T(256)S(1)} %copy-done.22), channel_id=1, source_target_pairs={{0,4},{4,0},{1,5},{5,1},{2,6},{6,2},{3,7},{7,3},{8,12},{12,8},{9,1... | collective-permute-start | bytes 3080 | tf_op jit(solution)/shard_map/ppermute | solution.py:23
  90.8 5.3 %copy-start.3 = (bf16[256,7168]{1,0:T(8,128)(2,1)S(1)}, bf16[256,7168]{1,0:T(8,128)(2,1)}, u32[]{:S(2)}) copy-start(bf16[256,7168]{1,0:T(8,128)(2,1)} %param.30) | copy-start | bytes 11010052
  90.8 5.7 %collective-permute-start.4 = (f32[128,256]{1,0:T(8,128)S(1)}, f32[128,256]{1,0:T(8,128)S(1)}, u32[]{:S(2)}, u32[]{:S(2)}) collective-permute-start(f32[128,256]{1,0:T(8,128)S(1)} %get-tuple-element.6), channel_id=1, source_target_pairs={{0,4},{4,0},{1,5},{5,1},{2,6},{6,2},{3,7},{7,3},{8,12},{12,8},{9,1... | collective-permute-start | bytes 393224 | tf_op jit(solution)/shard_map/ppermute | solution.py:23
  102.6 34.2 %all-to-all-start.4 = ((bf16[16,8,7296]{2,1,0:T(8,128)(2,1)}), bf16[16,8,7296]{2,1,0:T(8,128)(2,1)S(1)}, u32[]{:S(2)}, u32[]{:S(2)}) async-start(bf16[16,8,7296]{2,1,0:T(8,128)(2,1)} %fusion.10), calls=%async_computation.4 | async-start | bytes 3735552 | tf_op jit(solution)/shard_map/all_to_all | solution.py:19
  109.2 46.2 %collective-permute-start.8 = (bf16[3584,256]{1,0:T(8,128)(2,1)}, bf16[3584,256]{1,0:T(8,128)(2,1)}, u32[]{:S(2)}, u32[]{:S(2)}) collective-permute-start(bf16[3584,256]{1,0:T(8,128)(2,1)} %constant_dynamic-slice_fusion), channel_id=1, source_target_pairs={{0,4},{4,0},{1,5},{5,1},{2,6},{6,2},{3,7},{7,3},{8,12},{12,8},{9,1... | collective-permute-start | bytes 5505032 | tf_op jit(solution)/shard_map/ppermute | solution.py:23
  136.8 18.2 %copy-start.4 = (bf16[7168,256]{1,0:T(8,128)(2,1)S(1)}, bf16[7168,256]{1,0:T(8,128)(2,1)}, u32[]{:S(2)}) copy-start(bf16[7168,256]{1,0:T(8,128)(2,1)} %param.31) | copy-start | bytes 11010052
  158.0 10.5 %all-to-all-start.6 = ((bf16[8,32,256]{2,1,0:T(8,128)(2,1)}), bf16[8,32,256]{2,1,0:T(8,128)(2,1)S(1)}, u32[]{:S(2)}, u32[]{:S(2)}) async-start(bf16[8,32,256]{2,1,0:T(8,128)(2,1)} %bitcast.58), calls=%async_computation.6 | async-start | bytes 262144 | tf_op jit(solution)/shard_map/all_to_all | solution.py:19

commit v2 on v1

v2 whole, which is shorter than its diff:
```python
import functools
import math

import jax
import jax.numpy as jnp
from jax import lax
from jax.experimental import pallas as pl
from jax.experimental.pallas import tpu as pltpu
from jax.sharding import Mesh
from jax.sharding import PartitionSpec as P

D = 8192
CAP = 8
masked_score = -1e30
norm_eps = 1e-05
bf16 = jnp.bfloat16
f32 = jnp.float32
PLANE = ("z", "x")
NODE = ("z", "x", "core")
SWAP = [(0, 1), (1, 0)]


def exchange(x, axes):
    return lax.all_to_all(x, axes, split_axis=0, concat_axis=0, tiled=True)


def swapped(x):
    return lax.ppermute(x, "core", SWAP)


VMEM = pl.BlockSpec(memory_space=pltpu.VMEM)
SMEM = pl.BlockSpec(memory_space=pltpu.SMEM)
HBM = pl.BlockSpec(memory_space=pltpu.HBM)
CHIPS = 16
HEADS = 8
LEVEL = 128**-0.5 * math.log2(math.e)


def dot_rows(a, b):
    return lax.dot_general(a, b, (((1,), (1,)), ((), ())), preferred_element_type=f32)


def dot(a, b):
    return lax.dot_general(a, b, (((1,), (0,)), ((), ())), preferred_element_type=f32)


def iota(shape, dim):
    return lax.broadcasted_iota(jnp.int32, shape, dim)


def cut_kernel(core, after, gate, up, down, pair_ref, down_ref, sems):
    rows, hidden = gate.shape[0], down_ref.shape[0]
    half = pl.ds(pl.multiple_of((1 - core[0]) * hidden, 512), hidden)
    copies = [
        pltpu.make_async_copy(gate.at[:, half], pair_ref.at[0:rows], sems.at[0]),
        pltpu.make_async_copy(up.at[:, half], pair_ref.at[rows : 2 * rows], sems.at[1]),
        pltpu.make_async_copy(down.at[half, :], down_ref, sems.at[2]),
    ]
    for copy in copies:
        copy.start()
    for copy in copies:
        copy.wait()


def cut(core, after, gate, up, down):
    hidden = gate.shape[1] // 2
    return pl.pallas_call(
        cut_kernel,
        out_shape=(
            jax.ShapeDtypeStruct((2 * gate.shape[0], hidden), bf16),
            jax.ShapeDtypeStruct((hidden, down.shape[1]), bf16),
        ),
        in_specs=[SMEM] + [HBM] * 4,
        out_specs=(VMEM, VMEM),
        scratch_shapes=[pltpu.SemaphoreType.DMA((3,))],
        compiler_params=pltpu.CompilerParams(vmem_limit_bytes=56 << 20),
        cost_estimate=pl.CostEstimate(flops=0, bytes_accessed=11_000_000, transcendentals=0),
        name="cut",
    )(core, after, gate, up, down)


def split_kernel(core, *refs):
    sources, out_ref = refs[:4], refs[4]
    order = jnp.where(2 * iota((128, 256), 0) + core[0] == iota((128, 256), 1), 1.0, 0.0).astype(bf16)
    for i, ref in enumerate(sources):
        for start in range(0, ref.shape[0], 512):
            pair = jnp.concatenate([ref[start : start + 256], ref[start + 256 : start + 512]], axis=1)
            moved = dot(order, pair).astype(bf16)
            out_ref[i, start // 2 : start // 2 + 128] = moved[:, 0:128]
            out_ref[i, start // 2 + 128 : start // 2 + 256] = moved[:, 128:256]


def split_root(core, roots):
    sources = [flat(x) for x in roots]
    return pl.pallas_call(
        split_kernel,
        out_shape=jax.ShapeDtypeStruct((4, sources[0].shape[0] // 2, 128), bf16),
        in_specs=[SMEM] + [VMEM] * 4,
        out_specs=VMEM,
        compiler_params=pltpu.CompilerParams(vmem_limit_bytes=16 << 20),
        cost_estimate=pl.CostEstimate(flops=70_000_000, bytes_accessed=1_600_000, transcendentals=0),
        name="split_root",
    )(core, *sources)


def shared_kernel(scalars, q_ref, column_ref, row_ref, *refs):
    mids, (split, out_ref) = refs[:4], refs[4:]
    core = scalars[0]
    count = q_ref.shape[0]
    queries = q_ref[...]
    one = jnp.where(row_ref[...] == iota((128, count), 0), 1.0, 0.0).astype(bf16)
    picked = dot(one, queries).astype(bf16)
    levels, means = [], []
    for i in range(2):
        scores = dot_rows(picked[64 * i : 64 * i + 64], mids[2 * i][...])
        lane = iota(scores.shape, 1)
        usable = (lane % 2 == core) & (lane < 2 * scalars[1 + i])
        scores = jnp.where(usable, scores, masked_score)
        highest = jnp.max(scores, axis=1, keepdims=True)
        weights = jnp.where(usable, jnp.exp2((scores - highest) * LEVEL), 0.0)
        total = jnp.sum(weights, axis=1, keepdims=True)
        weighted = dot(weights.astype(bf16), mids[2 * i + 1][...])
        levels.append(highest * LEVEL + jnp.log2(total))
        means.append(weighted / total)
    level = jnp.concatenate(levels)
    mean = jnp.concatenate(means)
    eye = iota((128, 128), 0) == iota((128, 128), 1)
    level_row = jnp.sum(jnp.where(eye, level, 0.0), axis=0, keepdims=True)
    first = mean.astype(bf16)
    second = (mean - first.astype(f32)).astype(bf16)
    step = 256
    lanes = iota((64, 128), 1)
    diagonal = (lanes % 64) == iota((64, 128), 0)
    for at in range(0, count, step):
        here = column_ref[at : at + step] == iota((step, 128), 1)
        chosen = jnp.where(here, 1.0, 0.0).astype(bf16)
        known = dot(chosen, first) + dot(chosen, second)
        known_level = jnp.max(jnp.where(here, level_row, masked_score), axis=1, keepdims=True)
        rows = q_ref[at : at + step]
        near = dot_rows(rows, split[0])
        far = dot_rows(rows, split[2])
        highest = jnp.maximum(
            jnp.max(near, axis=1, keepdims=True), jnp.max(far, axis=1, keepdims=True)
        )
        top = jnp.maximum(highest * LEVEL, known_level)
        near = jnp.exp2(near * LEVEL - top)
        far = jnp.exp2(far * LEVEL - top)
        factor = jnp.exp2(known_level - top)
        total = factor + jnp.sum(near, axis=1, keepdims=True) + jnp.sum(far, axis=1, keepdims=True)
        weighted = (
            known * factor
            + dot(near.astype(bf16), split[1])
            + dot(far.astype(bf16), split[3])
        )
        result = weighted / total
        reached = top + jnp.log2(total)
        for j in range(step // 64):
            chip = at // 64 + j
            out_ref[chip, 0:64] = result[64 * j : 64 * j + 64].astype(bf16)
            line = jnp.sum(
                jnp.where(diagonal, reached[64 * j : 64 * j + 64], 0.0), axis=0, keepdims=True
            )
            large = line.astype(bf16).astype(f32)
            middle = (line - large).astype(bf16).astype(f32)
            small = line - large - middle
            pair = jnp.where(iota((1, 128), 1) < 64, large, middle)
            both = jnp.where(iota((16, 128), 0) == 0, pair, small)
            out_ref[chip, 64:80] = both.astype(bf16)


def flat(x):
    return x.reshape(-1, 128)


def shared_part(scalars, queries, column, row, mids, roots):
    return pl.pallas_call(
        shared_kernel,
        out_shape=jax.ShapeDtypeStruct((CHIPS, 80, 128), bf16),
        in_specs=[SMEM] + [VMEM] * 8,
        out_specs=VMEM,
        compiler_params=pltpu.CompilerParams(vmem_limit_bytes=32 << 20),
        cost_estimate=pl.CostEstimate(flops=800_000_000, bytes_accessed=4_300_000, transcendentals=1_200_000),
        name="shared_part",
    )(scalars, queries, column, row, *[flat(x) for x in mids], roots)


def own_kernel(scalars, q_ref, *refs):
    held, (high_ref, total_ref, mean_ref) = refs[:4], refs[4:]
    core, chip = scalars[0], scalars[1]
    for i in range(2):
        place = core if i == 0 else 1 - core
        for j in range(4):
            at = pl.ds(pl.multiple_of(place * 32 + 8 * j, 8), 8)
            rows = q_ref[pl.ds(pl.multiple_of(chip * 64 + place * 32 + 8 * j, 8), 8), :]
            scores = dot_rows(rows, held[2 * i][512 * j : 512 * j + 512])
            lane = iota(scores.shape, 1)
            usable = (lane % 2 == core) & (lane < 2 * scalars[2 + 4 * i + j])
            scores = jnp.where(usable, scores, masked_score)
            highest = jnp.max(scores, axis=1, keepdims=True)
            weights = jnp.where(usable, jnp.exp2((scores - highest) * LEVEL), 0.0)
            total = jnp.sum(weights, axis=1, keepdims=True)
            mean_ref[at, :] = dot(weights.astype(bf16), held[2 * i + 1][512 * j : 512 * j + 512])
            total_ref[at, :] = jnp.broadcast_to(total, (8, 128))
            high_ref[at, :] = jnp.broadcast_to(highest * LEVEL, (8, 128))


def own_part(scalars, queries, leaves):
    shape = jax.ShapeDtypeStruct((64, 128), f32)
    sources = [flat(x) for x in leaves]
    return pl.pallas_call(
        own_kernel,
        out_shape=(shape, shape, shape),
        in_specs=[SMEM] + [VMEM] * 5,
        out_specs=(VMEM, VMEM, VMEM),
        compiler_params=pltpu.CompilerParams(vmem_limit_bytes=16 << 20),
        cost_estimate=pl.CostEstimate(flops=17_000_000, bytes_accessed=400_000, transcendentals=40_000),
        name="own_part",
    )(scalars, queries, *sources)


def merge_kernel(parts_ref, high_ref, total_ref, mean_ref, out_ref):
    head = parts_ref[:, 64, :].astype(f32)
    small = parts_ref[:, 65, :].astype(f32)
    levels = jnp.transpose(head + pltpu.roll(head, 64, 1) + small)[0:64]
    own_level = high_ref[:, 0:1]
    top = jnp.maximum(jnp.max(levels, axis=1, keepdims=True), own_level)
    factors = jnp.exp2(levels - top)
    own_factor = jnp.exp2(own_level - top)
    total = jnp.sum(factors, axis=1, keepdims=True) + own_factor * total_ref[:, 0:1]
    weighted = own_factor * mean_ref[...]
    for chip in range(CHIPS):
        weighted += factors[:, chip : chip + 1] * parts_ref[chip, 0:64].astype(f32)
    attended = (weighted / total).astype(bf16)
    target, source = iota((64, 64), 0), iota((64, 64), 1)
    moved = jnp.where((target % 8) * 8 + target // 8 == source, 1.0, 0.0).astype(bf16)
    by_head = dot(moved, attended).astype(bf16)
    line = jnp.concatenate([by_head[8 * h : 8 * h + 8] for h in range(HEADS)], axis=1)
    for chip in range(CHIPS):
        out_ref[chip] = line


def merged(parts, high, total, mean):
    return pl.pallas_call(
        merge_kernel,
        out_shape=jax.ShapeDtypeStruct((CHIPS, 8, HEADS * 128), bf16),
        in_specs=[VMEM] * 4,
        out_specs=VMEM,
        compiler_params=pltpu.CompilerParams(vmem_limit_bytes=16 << 20),
        cost_estimate=pl.CostEstimate(flops=4_000_000, bytes_accessed=700_000, transcendentals=2_000),
        name="merged",
    )(parts, high, total, mean)


TILE = 1792


def gate_up_kernel(core, near_ref, far_ref, gain_ref, far_gain_ref, gate, up, pair, out, held, scaled, result, sems, out_sems):
    rows, hidden = gate.shape[0], pair.shape[1]
    copies, sent = [], []
    for i, near in enumerate((gate, up)):
        for at in range(0, hidden, TILE):
            start = pl.multiple_of(core[0] * hidden + at, TILE)
            far = pair.at[i * rows : (i + 1) * rows, at : at + TILE]
            for k, source in enumerate((near.at[:, pl.ds(start, TILE)], far)):
                copies.append(pltpu.make_async_copy(source, held.at[2 * i + k, :, at : at + TILE], sems.at[len(copies)]))
    for copy in copies:
        copy.start()

    def send(span):
        sent.append(pltpu.make_async_copy(result.at[:, span], out.at[:, span], out_sems.at[len(sent)]))
        sent[-1].start()

    squares = jnp.zeros((128, 1), f32)
    for i, (ref, gain) in enumerate(((near_ref, gain_ref), (far_ref, far_gain_ref))):
        stream = ref[...]
        squares += jnp.sum(stream * stream, axis=1, keepdims=True)
        scaled[i] = (stream * gain[...]).astype(bf16)
    large = squares.astype(bf16).astype(f32)
    middle = (squares - large).astype(bf16).astype(f32)
    small = squares - large - middle
    lane = iota((128, 128), 1)
    shown = jnp.where(lane == 0, large, jnp.where(lane == 1, middle, jnp.where(lane == 2, small, 0.0)))
    result[:, 2 * hidden :] = shown.astype(bf16)
    send(slice(2 * hidden, 2 * hidden + 128))
    for i in range(2):
        for at in range(0, hidden, TILE):
            done = 2 * len(sent) - 2
            copies[done].wait()
            copies[done + 1].wait()
            product = dot(scaled[0], held[2 * i, :, at : at + TILE]) + dot(scaled[1], held[2 * i + 1, :, at : at + TILE])
            result[:, i * hidden + at : i * hidden + at + TILE] = product.astype(bf16)
            send(slice(i * hidden + at, i * hidden + at + TILE))
    for copy in sent:
        copy.wait()


def gate_up(core, stream, stream_far, gain, gain_far, gate, up, pair):
    hidden = pair.shape[1]
    count = 2 * (hidden // TILE)
    return pl.pallas_call(
        gate_up_kernel,
        out_shape=jax.ShapeDtypeStruct((128, 2 * hidden + 128), bf16),
        in_specs=[SMEM] + [VMEM] * 4 + [HBM] * 3,
        out_specs=HBM,
        scratch_shapes=[
            pltpu.VMEM((4, 256, hidden), bf16),
            pltpu.VMEM((2, 128, 256), bf16),
            pltpu.VMEM((128, 2 * hidden + 128), bf16),
            pltpu.SemaphoreType.DMA((2 * count,)),
            pltpu.SemaphoreType.DMA((count + 1,)),
        ],
        compiler_params=pltpu.CompilerParams(vmem_limit_bytes=60 << 20),
        cost_estimate=pl.CostEstimate(flops=940_000_000, bytes_accessed=9_400_000, transcendentals=0),
        name="gate_up",
    )(core, stream, stream_far, gain, gain_far, gate, up, pair)


def load_kernel(core, weight, far_ref, near_out, far_out, token, sems):
    half = pl.ds(pl.multiple_of(core[0] * near_out.shape[0], 512), near_out.shape[0])
    copies = [
        pltpu.make_async_copy(weight.at[half, :], near_out, sems.at[0]),
        pltpu.make_async_copy(far_ref, far_out, sems.at[1]),
    ]
    for copy in copies:
        copy.start()
    token[...] = jnp.zeros_like(token)
    for copy in copies:
        copy.wait()


def load_down(core, weight, far):
    shape = jax.ShapeDtypeStruct(far.shape, bf16)
    return pl.pallas_call(
        load_kernel,
        out_shape=(shape, shape, jax.ShapeDtypeStruct((8, 128), f32)),
        in_specs=[SMEM, HBM, HBM],
        out_specs=(VMEM, VMEM, VMEM),
        scratch_shapes=[pltpu.SemaphoreType.DMA((2,))],
        compiler_params=pltpu.CompilerParams(vmem_limit_bytes=55 << 20),
        cost_estimate=pl.CostEstimate(flops=0, bytes_accessed=7_400_000, transcendentals=0),
        name="load_down",
    )(core, weight, far)


def activation_kernel(parts_ref, token, out_ref):
    hidden = out_ref.shape[2]

    def summed(at, width):
        total = parts_ref[0, :, at : at + width].astype(f32)
        for chip in range(1, CHIPS):
            total += parts_ref[chip, :, at : at + width].astype(f32)
        return total

    lane = iota((8, 128), 1)
    squares = jnp.sum(jnp.where(lane < 3, summed(2 * hidden, 128), 0.0), axis=1, keepdims=True)
    inverse = lax.rsqrt(squares / D + norm_eps)
    for at in range(0, hidden, 512):
        gate = summed(at, 512) * inverse
        upward = summed(hidden + at, 512) * inverse
        act = (gate / (1.0 + jnp.exp(-gate)) * upward).astype(bf16)
        for chip in range(CHIPS):
            out_ref[chip, :, at : at + 512] = act


def activation(parts, token):
    hidden = (parts.shape[2] - 128) // 2
    return pl.pallas_call(
        activation_kernel,
        out_shape=jax.ShapeDtypeStruct((CHIPS, 8, hidden), bf16),
        in_specs=[VMEM, HBM],
        out_specs=VMEM,
        compiler_params=pltpu.CompilerParams(vmem_limit_bytes=16 << 20),
        cost_estimate=pl.CostEstimate(flops=2_000_000, bytes_accessed=2_800_000, transcendentals=30_000),
        name="activation",
    )(parts, token)


def down_kernel(core, act_ref, near, far, out_ref):
    out_ref[core[0]] = dot(act_ref[...], near[...]).astype(bf16)
    out_ref[1 - core[0]] = dot(act_ref[...], far[...]).astype(bf16)


def down(core, acts, near, far):
    return pl.pallas_call(
        down_kernel,
        out_shape=jax.ShapeDtypeStruct((2, 128, far.shape[1]), bf16),
        in_specs=[SMEM, VMEM, VMEM, VMEM],
        out_specs=VMEM,
        compiler_params=pltpu.CompilerParams(vmem_limit_bytes=16 << 20),
        cost_estimate=pl.CostEstimate(flops=470_000_000, bytes_accessed=4_700_000, transcendentals=0),
        name="down",
    )(core, acts, near, far)


def on_device(
    queries,
    root_keys,
    root_values,
    mid_keys,
    mid_values,
    leaf_keys,
    leaf_values,
    mid_length,
    leaf_length,
    branch_mid,
    residual,
    norm_gain,
    out_weight,
    gate_weight,
    up_weight,
    down_weight,
):
    core = lax.axis_index("core")
    other = 1 - core
    chip = lax.axis_index(PLANE)
    head_size = queries.shape[2]
    hidden = gate_weight.shape[1] // 2

    halves = queries.reshape(4, 2, HEADS, head_size).transpose(1, 0, 2, 3)
    sent = jnp.broadcast_to(halves[None], (CHIPS, *halves.shape)).reshape(32, 4, HEADS, head_size)
    core_only = core.reshape(1)
    shared = (mid_keys, mid_values, root_keys, root_values)
    sent, shared = lax.optimization_barrier((sent, shared))
    gathered = exchange(sent, NODE).reshape(128 * HEADS, head_size)
    shared_far = [swapped(x) for x in shared]
    roots = split_root(core_only, (*shared[2:], *shared_far[2:]))

    nodes = jnp.stack([2 * chip + core, 2 * chip + other])
    routing = branch_mid[:, 0]
    place = jnp.arange(128)
    earlier = (routing[None, :] == routing[:, None]) & (place[None, :] < place[:, None])
    rank = jnp.sum(earlier.astype(jnp.int32), axis=1)
    slot = jnp.where(routing == nodes[0], rank, jnp.where(routing == nodes[1], CAP + rank, -CAP * CAP))
    slots = (slot[:, None] * HEADS + jnp.arange(HEADS)[None, :]).reshape(-1)

    payload = shared_part(
        jnp.concatenate([core_only, mid_length[nodes]]),
        gathered,
        slots[:, None],
        slots[None, :],
        (*shared[:2], *shared_far[:2]),
        roots,
    )
    leaves = (leaf_keys, leaf_values)
    payload, leaves = lax.optimization_barrier((payload, leaves))
    leaves = (*leaves, *[swapped(x) for x in leaves])
    scalars = jnp.concatenate([jnp.stack([core, chip]), leaf_length, swapped(leaf_length)])
    parts = exchange(payload, PLANE)
    own = own_part(scalars, gathered, leaves)
    attended = merged(parts, *own)
    attended_near = exchange(attended, PLANE).reshape(128, HEADS * head_size)
    pair, down_sent = cut(core_only, attended, gate_weight, up_weight, down_weight)
    attended_near, pair, down_sent = lax.optimization_barrier((attended_near, pair, down_sent))
    gain_far = swapped(norm_gain)
    attended_far, pair = lax.optimization_barrier((swapped(attended_near), pair))
    pair_far = swapped(pair)
    half_rows = out_weight.shape[0] // 2
    projected = jnp.dot(
        attended_near,
        lax.dynamic_slice_in_dim(out_weight, core * half_rows, half_rows, 0),
        preferred_element_type=f32,
    ) + jnp.dot(
        attended_far,
        lax.dynamic_slice_in_dim(out_weight, other * half_rows, half_rows, 0),
        preferred_element_type=f32,
    )
    share = projected.astype(bf16)
    stream = residual.astype(f32) + share.astype(f32)
    for step in (1, 2, 3):
        stream += lax.ppermute(share, "mp", [(i, (i + step) % 4) for i in range(4)]).astype(f32)
    stream_far = swapped(stream)
    payload = gate_up(
        core_only, stream, stream_far, norm_gain[None], gain_far[None], gate_weight, up_weight, pair_far
    )
    payload, down_sent = lax.optimization_barrier((payload, down_sent))
    parts = exchange(payload.reshape(CHIPS, 8, -1), PLANE)
    own_down, far_down, token = load_down(core_only, down_weight, swapped(down_sent))
    acts = exchange(activation(parts, token), PLANE).reshape(128, hidden)
    blocks = down(core_only, acts, own_down, far_down).reshape(8, 32, -1)
    arrived = exchange(blocks, ("core", "mp"))
    rows = lax.dynamic_slice_in_dim(stream, lax.axis_index("mp") * 32, 32, 0)
    return (rows + jnp.sum(arrived.astype(f32), axis=0)).astype(bf16)


def solution(mesh):
    fine = Mesh(mesh.devices.reshape(4, 4, 2, 4), ("z", "x", "core", "mp"))
    in_specs = (
        P(NODE, "mp", None),
        P(NODE, "mp", None),
        P(NODE, "mp", None),
        P(NODE, None, "mp", None),
        P(NODE, None, "mp", None),
        P(NODE, None, "mp", None),
        P(NODE, None, "mp", None),
        P(),
        P(NODE),
        P(),
        P(None, NODE),
        P(NODE),
        P("mp", NODE),
        P(NODE, "mp"),
        P(NODE, "mp"),
        P("mp", NODE),
    )
    return jax.shard_map(
        on_device, mesh=fine, in_specs=in_specs, out_specs=P("mp", NODE), check_vma=False
    )
```

time: 170 us -> 144 us (0.85)
  local copies, waits for them, and re-layouts: 37 us -> 9.11 us
  Pallas kernels: 0 us -> 27.2 us
  matrix products: 17.6 us -> 0.48 us
  waiting for transfers between devices: 51.6 us -> 45.8 us
  other arithmetic: 7.33 us -> 3.33 us
  starting transfers between devices: 37.3 us -> 39.5 us
    pallas_call x0 -> x9, Pallas kernels: none -> 27.2 us  [the longest x1 5.69 us: shared_part(): pl.pallas_call(shared_kernel, out_shape=jax.ShapeDtypeStruct((CHIPS, 80,...]
    dot_general x16 -> x2, matrix products: 17.6 us -> 0.48 us  [the longest x1 0.25 us: on_device(): jnp.dot(attended_far, lax.dynamic_slice_in_dim(out_weight, other * half_r...]
    dynamic_slice x6 -> x0, local copies, waits for them, and re-layouts: 17 us -> none  [the longest x3 8.35 us: of_head(): lax.dynamic_index_in_dim(x, head, x.ndim - 2, keepdims=False)]
    all_to_all x6 -> x5, waiting for transfers between devices: 51.6 us -> 37 us  [exchange(): return lax.all_to_all(x, axes, split_axis=0, concat_axis=0, tiled=True)]
    ppermute x0 -> x3, waiting for transfers between devices: none -> 5.6 us  [on_device(): lax.ppermute(share, 'mp', [(i, (i + step) % 4) for i in range(4)])]
    unnamed x65 -> x38, local copies, waits for them, and re-layouts: 10.6 us -> 6.57 us
    ppermute x0 -> x3, starting transfers between devices: none -> 3.84 us  [on_device(): lax.ppermute(share, 'mp', [(i, (i + step) % 4) for i in range(4)])]
    ppermute x9 -> x12, waiting for transfers between devices: 0.02 us -> 3.24 us  [swapped(): return lax.ppermute(x, 'core', SWAP)]
  transfers between devices with their start and end apart: 15 -> 20, of which waited for: 6 -> 11; matrix products, arithmetic and copies ran while one was open for 15% -> 2% of each run, Pallas kernels for 0% -> 9%
where the time goes in v2:
time: 144 us; the launch traced here: 143 us
  waiting for transfers between devices  45.8 us (32%)
  starting transfers between devices  39.5 us (27%)
  Pallas kernels  27.2 us (19%)
  blocking collectives  17.5 us (12%)
  local copies, waits for them, and re-layouts  9.11 us (6%)
  other arithmetic  3.33 us (2%)
    all_to_all x5, waiting for transfers between devices, exchange(): return lax.all_to_all(x, axes, split_axis=0, concat_axis=0, tiled=True)  37 us
    all_to_all x5, starting transfers between devices, exchange(): return lax.all_to_all(x, axes, split_axis=0, concat_axis=0, tiled=True)  29.1 us
    all_to_all x1, blocking collectives, exchange(): return lax.all_to_all(x, axes, split_axis=0, concat_axis=0, tiled=True)  17.5 us
    ppermute x12, starting transfers between devices, swapped(): return lax.ppermute(x, 'core', SWAP)  6.59 us
    unnamed x38, local copies, waits for them, and re-layouts  6.57 us
    pallas_call x1, Pallas kernels, shared_part(): pl.pallas_call(shared_kernel, out_shape=jax.ShapeDtypeStruct((CHIPS, 80,...  5.69 us
    pallas_call x1, Pallas kernels, gate_up(): pl.pallas_call(gate_up_kernel, out_shape=jax.ShapeDtypeStruct((128, 2 * h...  5.66 us
    ppermute x3, waiting for transfers between devices, on_device(): lax.ppermute(share, 'mp', [(i, (i + step) % 4) for i in range(4)])  5.6 us
  transfers between devices with their start and end apart: 20, of which 11 were waited for; matrix products, arithmetic and copies ran while one was open for 2% of the time, Pallas kernels for 9%

profile of v2, /device:TPU:1, one launch (start us, length us, event | category | flops | bytes accessed | tf_op | source)
XLA Modules:
  0.0 143.2 jit_solution(11334112572223063131)
XLA Ops:
  0.0 0.9 copy.20
  0.9 0.7 broadcast_in_dim.10
  1.6 9.4 %all-to-all-start = ((bf16[32,4,8,128]{3,2,1,0:T(8,128)(2,1)}), bf16[32,4,8,128]{3,2,1,0:T(8,128)(2,1)S(1)}, u32[]{:S(2)}, u32[]{:S(2)}) async-start(bf16[32,4,8,128]{3,2,1,0:T(8,128)(2,1)} %bitcast.6), calls=%async_computation | async-start | bytes 524288 | tf_op jit(solution)/shard_map/all_to_all | solution.py:24
  11.1 0.3 collective-permute-start.2
  11.4 0.3 collective-permute-start.3
  11.7 0.2 collective-permute-start
  11.9 0.3 collective-permute-start.1
  12.2 0.9 convert_reduce_fusion.1
  13.1 0.7 fusion.9
  13.8 0.1 iota_add_fusion
  13.8 0.1 fusion.8
  13.9 0.1 add.105.row_ref
  14.0 0.2 add.115.column_ref
  14.2 0.6 gather_fusion
  14.9 0.1 pad_add_fusion.scalars
  15.0 0.7 copy-done.7
  15.7 0.7 copy-done.9
  16.4 0.9 copy-done.5
  17.3 0.9 copy-done.6
  18.3 0.9 copy-done.8
  19.2 0.9 copy-done.10
  20.2 0.3 split_root.1.refs_4_
  20.6 5.7 %shared_part.1 = bf16[16,80,128]{2,1,0:T(8,128)(2,1)} custom-call(s32[3]{0:T(128)S(1)} %pad_add_fusion.scalars, bf16[1024,128]{1,0:T(8,128)(2,1)S(1)} %bitcast.42, s32[1024,1]{1,0:T(8,128)S(1)} %add.115.column_ref, s32[1,1024]{1,0:T(1,128)S(1)} %add.105.row_ref, bf16[2048,128]{1,0:T(8,128)(2,1)S(1)} %bitcast.44, bf16[2048,128]{1,0:T(8,128)(2,1)S(1)} %bitcast.45, ...), custom_call_target="tpu_custom_call" | custom-call | flops 800000000 | bytes 4300000 | tf_op jit(solution)/shard_map/shared_part/pallas_call | solution.py:176
  26.2 0.2 collective-permute-start.5
  26.5 0.3 collective-permute-start.6
  26.8 6.7 %all-to-all-start.1 = ((bf16[16,80,128]{2,1,0:T(8,128)(2,1)}), bf16[16,80,128]{2,1,0:T(8,128)(2,1)S(1)}, u32[]{:S(2)}, u32[]{:S(2)}) async-start(bf16[16,80,128]{2,1,0:T(8,128)(2,1)} %shared_part.1), calls=%async_computation.1 | async-start | bytes 655360 | tf_op jit(solution)/shard_map/all_to_all | solution.py:24
  33.5 0.7 collective-permute-start.4
  34.2 0.8 collective-permute-done.4
  35.0 0.1 pad_add_fusion.1.scalars
  35.1 3.2 %own_part.1 = (f32[64,128]{1,0:T(8,128)S(1)}, f32[64,128]{1,0:T(8,128)S(1)}, f32[64,128]{1,0:T(8,128)S(1)}) custom-call(s32[10]{0:T(128)S(1)} %pad_add_fusion.1.scalars, bf16[1024,128]{1,0:T(8,128)(2,1)S(1)} %bitcast.43, bf16[2048,128]{1,0:T(8,128)(2,1)} %bitcast.20.refs_0_, bf16[2048,128]{1,0:T(8,128)(2,1)} %bitcast.21.refs_1_, ...), custom_call_target="tpu_custom_call" | custom-call | flops 17000000 | bytes 400000 | tf_op jit(solution)/shard_map/own_part/pallas_call | solution.py:210
  38.3 4.0 %all-to-all-done.1.parts_ref = bf16[16,80,128]{2,1,0:T(8,128)(2,1)S(1)} async-done(((bf16[16,80,128]{2,1,0:T(8,128)(2,1)}), bf16[16,80,128]{2,1,0:T(8,128)(2,1)S(1)}, u32[]{:S(2)}, u32[]{:S(2)}) %all-to-all-start.1) | async-done | bytes 327712 | tf_op jit(solution)/shard_map/all_to_all | solution.py:24
  42.3 1.7 %merged.1.after = bf16[16,8,1024]{2,1,0:T(8,128)(2,1)} custom-call(bf16[16,80,128]{2,1,0:T(8,128)(2,1)S(1)} %all-to-all-done.1.parts_ref, f32[64,128]{1,0:T(8,128)S(1)} %get-tuple-element.36.high_ref, f32[64,128]{1,0:T(8,128)S(1)} %get-tuple-element.37.total_ref, f32[64,128]{1,0:T(8,128)S(1)} %get-tuple-element.38.mean_ref), custom_call_target="tpu_custom_call" | custom-call | flops 4000000 | bytes 700000 | tf_op jit(solution)/shard_map/merged/pallas_call | solution.py:243
  44.0 3.5 %all-to-all-start.2 = ((bf16[16,8,1024]{2,1,0:T(8,128)(2,1)}), bf16[16,8,1024]{2,1,0:T(8,128)(2,1)S(1)}, u32[]{:S(2)}, u32[]{:S(2)}) async-start(bf16[16,8,1024]{2,1,0:T(8,128)(2,1)} %merged.1.after), calls=%async_computation.2 | async-start | bytes 524288 | tf_op jit(solution)/shard_map/all_to_all | solution.py:24
  47.5 5.2 %cut.1 = (bf16[512,3584]{1,0:T(8,128)(2,1)}, bf16[3584,256]{1,0:T(8,128)(2,1)}) custom-call(s32[1]{0:T(128)} %bitcast.core, bf16[16,8,1024]{2,1,0:T(8,128)(2,1)} %merged.1.after, bf16[256,7168]{1,0:T(8,128)(2,1)} %gate.3, bf16[256,7168]{1,0:T(8,128)(2,1)} %up.3, bf16[7168,256]{1,0:T(8,128)(2,1)} %weight.1), custom_call_target="tpu_custom_call" | custom-call | bytes 11000000 | tf_op jit(solution)/shard_map/cut/pallas_call | solution.py:67
  52.7 2.3 %all-to-all-done.2 = bf16[16,8,1024]{2,1,0:T(8,128)(2,1)S(1)} async-done(((bf16[16,8,1024]{2,1,0:T(8,128)(2,1)}), bf16[16,8,1024]{2,1,0:T(8,128)(2,1)S(1)}, u32[]{:S(2)}, u32[]{:S(2)}) %all-to-all-start.2) | async-done | bytes 262176 | tf_op jit(solution)/shard_map/all_to_all | solution.py:24
  55.0 2.7 %collective-permute-start.7 = (bf16[128,1024]{1,0:T(8,128)(2,1)S(1)}, bf16[128,1024]{1,0:T(8,128)(2,1)S(1)}, u32[]{:S(2)}, u32[]{:S(2)}) collective-permute-start(bf16[128,1024]{1,0:T(8,128)(2,1)S(1)} %bitcast.53), channel_id=1, source_target_pairs={{0,4},{4,0},{1,5},{5,1},{2,6},{6,2},{3,7},{7,3},{8,12},{12,8},{9,1... | collective-permute-start | bytes 786440 | tf_op jit(solution)/shard_map/ppermute | solution.py:28
  57.7 1.2 collective-permute-done.7
  58.8 0.4 collective-permute-start.13
  59.2 0.2 fusion.2
  59.4 0.2 fusion
  59.7 2.8 %collective-permute-start.10 = (bf16[128,256]{1,0:T(8,128)(2,1)S(1)}, bf16[128,256]{1,0:T(8,128)(2,1)S(1)}, u32[]{:S(2)}, u32[]{:S(2)}) collective-permute-start(bf16[128,256]{1,0:T(8,128)(2,1)S(1)} %fusion), channel_id=1, source_target_pairs={{0,3},{1,0},{2,1},{3,2},{4,7},{5,4},{6,5},{7,6},{8,11},{9,8},{10,9... | collective-permute-start | bytes 196616 | tf_op jit(solution)/shard_map/ppermute | solution.py:470
  62.5 0.3 collective-permute-start.9
  62.8 0.7 collective-permute-start.8
  63.5 0.3 collective-permute-done.10
  63.8 3.4 %collective-permute-done.9 = bf16[128,256]{1,0:T(8,128)(2,1)S(1)} collective-permute-done((bf16[128,256]{1,0:T(8,128)(2,1)S(1)}, bf16[128,256]{1,0:T(8,128)(2,1)S(1)}, u32[]{:S(2)}, u32[]{:S(2)}) %collective-permute-start.9) | collective-permute-done | bytes 65568 | tf_op jit(solution)/shard_map/ppermute | solution.py:470
  67.2 2.0 %collective-permute-done.8 = bf16[128,256]{1,0:T(8,128)(2,1)S(1)} collective-permute-done((bf16[128,256]{1,0:T(8,128)(2,1)S(1)}, bf16[128,256]{1,0:T(8,128)(2,1)S(1)}, u32[]{:S(2)}, u32[]{:S(2)}) %collective-permute-start.8) | collective-permute-done | bytes 65568 | tf_op jit(solution)/shard_map/ppermute | solution.py:470
  69.2 0.9 collective-permute-start.11
  70.1 0.1 collective-permute-start.12
  70.2 1.0 collective-permute-done.12
  71.2 0.5 copy-done.17
  71.8 0.1 copy-done.14
  71.8 5.7 %gate_up.1 = bf16[128,7296]{1,0:T(8,128)(2,1)} custom-call(s32[1]{0:T(128)} %bitcast.core, f32[128,256]{1,0:T(8,128)} %copy-done.13, f32[128,256]{1,0:T(8,128)} %copy-done.14, f32[1,256]{1,0:T(1,128)} %bitcast.56, f32[1,256]{1,0:T(1,128)} %bitcast.57, bf16[256,7168]{1,0:T(8,128)(2,1)} %gate.3, bf16[256,7168]{1,0:T(8,128)(2,1)} %up.3, ...), custom_call_target="tpu_custom_call" | custom-call | flops 940000000 | bytes 9400000 | tf_op jit(solution)/shard_map/gate_up/pallas_call | solution.py:300
  77.5 0.3 collective-permute-start.14
  77.8 3.7 %all-to-all-start.3 = ((bf16[16,8,7296]{2,1,0:T(8,128)(2,1)}), bf16[16,8,7296]{2,1,0:T(8,128)(2,1)S(1)}, u32[]{:S(2)}, u32[]{:S(2)}) async-start(bf16[16,8,7296]{2,1,0:T(8,128)(2,1)} %bitcast.52), calls=%async_computation.3 | async-start | bytes 3735552 | tf_op jit(solution)/shard_map/all_to_all | solution.py:24
  81.5 0.2 collective-permute-done.14.far_ref
  81.7 3.9 %load_down.1 = (bf16[3584,256]{1,0:T(8,128)(2,1)}, bf16[3584,256]{1,0:T(8,128)(2,1)}, f32[8,128]{1,0:T(8,128)}) custom-call(s32[1]{0:T(128)} %bitcast.core, bf16[7168,256]{1,0:T(8,128)(2,1)} %weight.1, bf16[3584,256]{1,0:T(8,128)(2,1)} %collective-permute-done.14.far_ref), custom_call_target="tpu_custom_call" | custom-call | bytes 7400000 | tf_op jit(solution)/shard_map/load_down/pallas_call | solution.py:333
  85.6 25.5 %all-to-all-done.3.parts_ref = bf16[16,8,7296]{2,1,0:T(8,128)(2,1)S(1)} async-done(((bf16[16,8,7296]{2,1,0:T(8,128)(2,1)}), bf16[16,8,7296]{2,1,0:T(8,128)(2,1)S(1)}, u32[]{:S(2)}, u32[]{:S(2)}) %all-to-all-start.3) | async-done | bytes 1867808 | tf_op jit(solution)/shard_map/all_to_all | solution.py:24
  111.1 0.7 copy-done.11
  111.8 0.3 activation.1
  112.1 17.5 %all_to_all.30 = bf16[16,8,3584]{2,1,0:T(8,128)(2,1)S(1)} all-to-all(bf16[16,8,3584]{2,1,0:T(8,128)(2,1)S(1)} %activation.1), channel_id=1, replica_groups=mesh['z'=4,'x'=4,'core'=2,'mp'=4] {'z','x'}, dimensions={0} | all-to-all | bytes 1835008 | tf_op jit(solution)/shard_map/all_to_all | solution.py:24
  129.6 1.3 down.3
  130.9 5.7 %all-to-all-start.5 = ((bf16[8,32,256]{2,1,0:T(8,128)(2,1)}), bf16[8,32,256]{2,1,0:T(8,128)(2,1)S(1)}, u32[]{:S(2)}, u32[]{:S(2)}) async-start(bf16[8,32,256]{2,1,0:T(8,128)(2,1)} %bitcast.29), calls=%async_computation.5 | async-start | bytes 262144 | tf_op jit(solution)/shard_map/all_to_all | solution.py:24
  136.6 5.2 %all-to-all-done.5 = bf16[8,32,256]{2,1,0:T(8,128)(2,1)S(1)} async-done(((bf16[8,32,256]{2,1,0:T(8,128)(2,1)}), bf16[8,32,256]{2,1,0:T(8,128)(2,1)S(1)}, u32[]{:S(2)}, u32[]{:S(2)}) %all-to-all-start.5) | async-done | bytes 131104 | tf_op jit(solution)/shard_map/all_to_all | solution.py:24
  141.8 1.4 add_convert_fusion
  (41 shorter events, 0.2 us)
Async XLA Ops:
  0.0 59.2 %copy-start = (bf16[2048,256]{1,0:T(8,128)(2,1)S(1)}, bf16[2048,256]{1,0:T(8,128)(2,1)}, u32[]{:S(2)}) copy-start(bf16[2048,256]{1,0:T(8,128)(2,1)} %param.28) | copy-start | bytes 3145732
  0.0 20.5 %copy-start.4 = (bf16[1,1024,2,128]{3,2,1,0:T(2,128)(2,1)S(1)}, bf16[1,1024,2,128]{3,2,1,0:T(2,128)(2,1)}, u32[]{:S(2)}) copy-start(bf16[1,1024,2,128]{3,2,1,0:T(2,128)(2,1)} %param.20) | copy-start | bytes 1572868
  0.0 20.5 %copy-start.3 = (bf16[1,1024,2,128]{3,2,1,0:T(2,128)(2,1)S(1)}, bf16[1,1024,2,128]{3,2,1,0:T(2,128)(2,1)}, u32[]{:S(2)}) copy-start(bf16[1,1024,2,128]{3,2,1,0:T(2,128)(2,1)} %param.19) | copy-start | bytes 1572868
  0.0 14.2 %copy-start.12 = (s32[32]{0:T(128)S(1)}, s32[32]{0:T(128)}, u32[]{:S(2)}) copy-start(s32[32]{0:T(128)} %param.23) | copy-start | bytes 388
  1.6 18.9 %all-to-all-start = ((bf16[32,4,8,128]{3,2,1,0:T(8,128)(2,1)}), bf16[32,4,8,128]{3,2,1,0:T(8,128)(2,1)S(1)}, u32[]{:S(2)}, u32[]{:S(2)}) async-start(bf16[32,4,8,128]{3,2,1,0:T(8,128)(2,1)} %bitcast.6), calls=%async_computation | async-start | bytes 524288 | tf_op jit(solution)/shard_map/all_to_all | solution.py:24
  11.1 3.9 %collective-permute-start.2 = (bf16[512,2,128]{2,1,0:T(2,128)(2,1)}, bf16[512,2,128]{2,1,0:T(2,128)(2,1)S(1)}, u32[]{:S(2)}, u32[]{:S(2)}) collective-permute-start(bf16[512,2,128]{2,1,0:T(2,128)(2,1)} %param.17), channel_id=1, source_target_pairs={{0,4},{4,0},{1,5},{5,1},{2,6},{6,2},{3,7},{7,3},{8,12},{12,8},{9,1... | collective-permute-start | bytes 786440 | tf_op jit(solution)/shard_map/ppermute | solution.py:28
  11.4 4.3 %collective-permute-start.3 = (bf16[512,2,128]{2,1,0:T(2,128)(2,1)}, bf16[512,2,128]{2,1,0:T(2,128)(2,1)S(1)}, u32[]{:S(2)}, u32[]{:S(2)}) collective-permute-start(bf16[512,2,128]{2,1,0:T(2,128)(2,1)} %param.18), channel_id=1, source_target_pairs={{0,4},{4,0},{1,5},{5,1},{2,6},{6,2},{3,7},{7,3},{8,12},{12,8},{9,1... | collective-permute-start | bytes 786440 | tf_op jit(solution)/shard_map/ppermute | solution.py:28
  11.7 8.8 %collective-permute-start = (bf16[1,1024,2,128]{3,2,1,0:T(2,128)(2,1)}, bf16[1,1024,2,128]{3,2,1,0:T(2,128)(2,1)}, u32[]{:S(2)}, u32[]{:S(2)}) collective-permute-start(bf16[1,1024,2,128]{3,2,1,0:T(2,128)(2,1)} %param.19), channel_id=1, source_target_pairs={{0,4},{4,0},{1,5},{5,1},{2,6},{6,2},{3,7},{7,3},{8,12},{12,8},{9,1... | collective-permute-start | bytes 1572872 | tf_op jit(solution)/shard_map/ppermute | solution.py:28
  11.9 8.6 %collective-permute-start.1 = (bf16[1,1024,2,128]{3,2,1,0:T(2,128)(2,1)}, bf16[1,1024,2,128]{3,2,1,0:T(2,128)(2,1)}, u32[]{:S(2)}, u32[]{:S(2)}) collective-permute-start(bf16[1,1024,2,128]{3,2,1,0:T(2,128)(2,1)} %param.20), channel_id=1, source_target_pairs={{0,4},{4,0},{1,5},{5,1},{2,6},{6,2},{3,7},{7,3},{8,12},{12,8},{9,1... | collective-permute-start | bytes 1572872 | tf_op jit(solution)/shard_map/ppermute | solution.py:28
  15.0 0.7 copy-start.7
  15.7 0.7 copy-start.9
  16.4 0.9 copy-start.5
  17.3 0.9 copy-start.6
  18.3 0.9 copy-start.8
  19.2 0.9 copy-start.10
  20.5 12.9 %copy-start.18 = (s32[4]{0:T(128)S(1)}, s32[4]{0:T(128)}, u32[]{:S(2)}) copy-start(s32[4]{0:T(128)} %param.24) | copy-start | bytes 52
  26.2 8.8 %collective-permute-start.5 = (bf16[4,256,2,128]{3,2,1,0:T(2,128)(2,1)}, bf16[4,256,2,128]{3,2,1,0:T(2,128)(2,1)S(1)}, u32[]{:S(2)}, u32[]{:S(2)}) collective-permute-start(bf16[4,256,2,128]{3,2,1,0:T(2,128)(2,1)} %param.21), channel_id=1, source_target_pairs={{0,4},{4,0},{1,5},{5,1},{2,6},{6,2},{3,7},{7,3},{8,12},{12,8},{9,1... | collective-permute-start | bytes 1572872 | tf_op jit(solution)/shard_map/ppermute | solution.py:28
  26.5 8.6 %collective-permute-start.6 = (bf16[4,256,2,128]{3,2,1,0:T(2,128)(2,1)}, bf16[4,256,2,128]{3,2,1,0:T(2,128)(2,1)S(1)}, u32[]{:S(2)}, u32[]{:S(2)}) collective-permute-start(bf16[4,256,2,128]{3,2,1,0:T(2,128)(2,1)} %param.22), channel_id=1, source_target_pairs={{0,4},{4,0},{1,5},{5,1},{2,6},{6,2},{3,7},{7,3},{8,12},{12,8},{9,1... | collective-permute-start | bytes 1572872 | tf_op jit(solution)/shard_map/ppermute | solution.py:28
  26.8 15.5 %all-to-all-start.1 = ((bf16[16,80,128]{2,1,0:T(8,128)(2,1)}), bf16[16,80,128]{2,1,0:T(8,128)(2,1)S(1)}, u32[]{:S(2)}, u32[]{:S(2)}) async-start(bf16[16,80,128]{2,1,0:T(8,128)(2,1)} %shared_part.1), calls=%async_computation.1 | async-start | bytes 655360 | tf_op jit(solution)/shard_map/all_to_all | solution.py:24
  33.5 1.5 %collective-permute-start.4 = (s32[4]{0:T(128)S(1)}, s32[4]{0:T(128)S(1)}, u32[]{:S(2)}, u32[]{:S(2)}) collective-permute-start(s32[4]{0:T(128)S(1)} %copy-done.18), channel_id=1, source_target_pairs={{0,4},{4,0},{1,5},{5,1},{2,6},{6,2},{3,7},{7,3},{8,12},{12,8},{9,1... | collective-permute-start | bytes 56 | tf_op jit(solution)/shard_map/ppermute | solution.py:28
  44.0 11.0 %all-to-all-start.2 = ((bf16[16,8,1024]{2,1,0:T(8,128)(2,1)}), bf16[16,8,1024]{2,1,0:T(8,128)(2,1)S(1)}, u32[]{:S(2)}, u32[]{:S(2)}) async-start(bf16[16,8,1024]{2,1,0:T(8,128)(2,1)} %merged.1.after), calls=%async_computation.2 | async-start | bytes 524288 | tf_op jit(solution)/shard_map/all_to_all | solution.py:24
  52.7 16.5 %copy-start.15 = (bf16[128,256]{1,0:T(8,128)(2,1)S(1)}, bf16[128,256]{1,0:T(8,128)(2,1)}, u32[]{:S(2)}) copy-start(bf16[128,256]{1,0:T(8,128)(2,1)} %param.26) | copy-start | bytes 196612
  52.7 17.4 %copy-start.16 = (f32[256]{0:T(256)S(1)}, f32[256]{0:T(256)}, u32[]{:S(2)}) copy-start(f32[256]{0:T(256)} %param.27) | copy-start | bytes 3076
  55.0 3.8 %collective-permute-start.7 = (bf16[128,1024]{1,0:T(8,128)(2,1)S(1)}, bf16[128,1024]{1,0:T(8,128)(2,1)S(1)}, u32[]{:S(2)}, u32[]{:S(2)}) collective-permute-start(bf16[128,1024]{1,0:T(8,128)(2,1)S(1)} %bitcast.53), channel_id=1, source_target_pairs={{0,4},{4,0},{1,5},{5,1},{2,6},{6,2},{3,7},{7,3},{8,12},{12,8},{9,1... | collective-permute-start | bytes 786440 | tf_op jit(solution)/shard_map/ppermute | solution.py:28
  58.8 12.4 %collective-permute-start.13 = (bf16[512,3584]{1,0:T(8,128)(2,1)}, bf16[512,3584]{1,0:T(8,128)(2,1)}, u32[]{:S(2)}, u32[]{:S(2)}) collective-permute-start(bf16[512,3584]{1,0:T(8,128)(2,1)} %get-tuple-element.44), channel_id=1, source_target_pairs={{0,4},{4,0},{1,5},{5,1},{2,6},{6,2},{3,7},{7,3},{8,12},{12,8},{9,1... | collective-permute-start | bytes 11010056 | tf_op jit(solution)/shard_map/ppermute | solution.py:28
  59.7 4.1 %collective-permute-start.10 = (bf16[128,256]{1,0:T(8,128)(2,1)S(1)}, bf16[128,256]{1,0:T(8,128)(2,1)S(1)}, u32[]{:S(2)}, u32[]{:S(2)}) collective-permute-start(bf16[128,256]{1,0:T(8,128)(2,1)S(1)} %fusion), channel_id=1, source_target_pairs={{0,3},{1,0},{2,1},{3,2},{4,7},{5,4},{6,5},{7,6},{8,11},{9,8},{10,9... | collective-permute-start | bytes 196616 | tf_op jit(solution)/shard_map/ppermute | solution.py:470
  62.5 4.7 %collective-permute-start.9 = (bf16[128,256]{1,0:T(8,128)(2,1)S(1)}, bf16[128,256]{1,0:T(8,128)(2,1)S(1)}, u32[]{:S(2)}, u32[]{:S(2)}) collective-permute-start(bf16[128,256]{1,0:T(8,128)(2,1)S(1)} %fusion), channel_id=1, source_target_pairs={{0,2},{1,3},{2,0},{3,1},{4,6},{5,7},{6,4},{7,5},{8,10},{9,11},{10,... | collective-permute-start | bytes 196616 | tf_op jit(solution)/shard_map/ppermute | solution.py:470
  62.8 6.3 %collective-permute-start.8 = (bf16[128,256]{1,0:T(8,128)(2,1)S(1)}, bf16[128,256]{1,0:T(8,128)(2,1)S(1)}, u32[]{:S(2)}, u32[]{:S(2)}) collective-permute-start(bf16[128,256]{1,0:T(8,128)(2,1)S(1)} %fusion), channel_id=1, source_target_pairs={{0,1},{1,2},{2,3},{3,0},{4,5},{5,6},{6,7},{7,4},{8,9},{9,10},{10,1... | collective-permute-start | bytes 196616 | tf_op jit(solution)/shard_map/ppermute | solution.py:470
  69.2 2.0 %copy-start.13 = (f32[128,256]{1,0:T(8,128)}, f32[128,256]{1,0:T(8,128)S(1)}, u32[]{:S(2)}) copy-start(f32[128,256]{1,0:T(8,128)S(1)} %convert_add_fusion.near_ref) | copy-start | bytes 393220
  69.2 2.0 %collective-permute-start.11 = (f32[128,256]{1,0:T(8,128)S(1)}, f32[128,256]{1,0:T(8,128)S(1)}, u32[]{:S(2)}, u32[]{:S(2)}) collective-permute-start(f32[128,256]{1,0:T(8,128)S(1)} %convert_add_fusion.near_ref), channel_id=1, source_target_pairs={{0,4},{4,0},{1,5},{5,1},{2,6},{6,2},{3,7},{7,3},{8,12},{12,8},{9,1... | collective-permute-start | bytes 393224 | tf_op jit(solution)/shard_map/ppermute | solution.py:28
  70.1 1.1 collective-permute-start.12
  71.2 0.6 copy-start.17
  71.2 0.7 copy-start.14
  77.5 4.2 %collective-permute-start.14 = (bf16[3584,256]{1,0:T(8,128)(2,1)}, bf16[3584,256]{1,0:T(8,128)(2,1)}, u32[]{:S(2)}, u32[]{:S(2)}) collective-permute-start(bf16[3584,256]{1,0:T(8,128)(2,1)} %get-tuple-element.47), channel_id=1, source_target_pairs={{0,4},{4,0},{1,5},{5,1},{2,6},{6,2},{3,7},{7,3},{8,12},{12,8},{9,1... | collective-permute-start | bytes 5505032 | tf_op jit(solution)/shard_map/ppermute | solution.py:28
  77.8 33.3 %all-to-all-start.3 = ((bf16[16,8,7296]{2,1,0:T(8,128)(2,1)}), bf16[16,8,7296]{2,1,0:T(8,128)(2,1)S(1)}, u32[]{:S(2)}, u32[]{:S(2)}) async-start(bf16[16,8,7296]{2,1,0:T(8,128)(2,1)} %bitcast.52), calls=%async_computation.3 | async-start | bytes 3735552 | tf_op jit(solution)/shard_map/all_to_all | solution.py:24
  111.1 0.7 copy-start.11
  111.8 17.8 %copy-start.1 = (bf16[3584,256]{1,0:T(8,128)(2,1)S(1)}, bf16[3584,256]{1,0:T(8,128)(2,1)}, u32[]{:S(2)}) copy-start(bf16[3584,256]{1,0:T(8,128)(2,1)} %get-tuple-element.49.near) | copy-start | bytes 5505028
  111.8 17.8 %copy-start.2 = (bf16[3584,256]{1,0:T(8,128)(2,1)S(1)}, bf16[3584,256]{1,0:T(8,128)(2,1)}, u32[]{:S(2)}) copy-start(bf16[3584,256]{1,0:T(8,128)(2,1)} %get-tuple-element.50.far) | copy-start | bytes 5505028
  130.9 10.9 %all-to-all-start.5 = ((bf16[8,32,256]{2,1,0:T(8,128)(2,1)}), bf16[8,32,256]{2,1,0:T(8,128)(2,1)S(1)}, u32[]{:S(2)}, u32[]{:S(2)}) async-start(bf16[8,32,256]{2,1,0:T(8,128)(2,1)} %bitcast.29), calls=%async_computation.5 | async-start | bytes 262144 | tf_op jit(solution)/shard_map/all_to_all | solution.py:24

commit v3 on v2

--- a/solution.py
+++ b/solution.py
@@ -48,7 +48,7 @@
     return lax.broadcasted_iota(jnp.int32, shape, dim)
 
 
-def cut_kernel(core, after, gate, up, down, pair_ref, down_ref, sems):
+def cut_kernel(core, gate, up, down, pair_ref, down_ref, sems):
     rows, hidden = gate.shape[0], down_ref.shape[0]
     half = pl.ds(pl.multiple_of((1 - core[0]) * hidden, 512), hidden)
     copies = [
@@ -62,7 +62,7 @@
         copy.wait()
 
 
-def cut(core, after, gate, up, down):
+def cut(core, gate, up, down):
     hidden = gate.shape[1] // 2
     return pl.pallas_call(
         cut_kernel,
@@ -70,13 +70,13 @@
             jax.ShapeDtypeStruct((2 * gate.shape[0], hidden), bf16),
             jax.ShapeDtypeStruct((hidden, down.shape[1]), bf16),
         ),
-        in_specs=[SMEM] + [HBM] * 4,
+        in_specs=[SMEM] + [HBM] * 3,
         out_specs=(VMEM, VMEM),
         scratch_shapes=[pltpu.SemaphoreType.DMA((3,))],
         compiler_params=pltpu.CompilerParams(vmem_limit_bytes=56 << 20),
         cost_estimate=pl.CostEstimate(flops=0, bytes_accessed=11_000_000, transcendentals=0),
         name="cut",
-    )(core, after, gate, up, down)
+    )(core, gate, up, down)
 
 
 def split_kernel(core, *refs):
@@ -416,8 +416,8 @@
     head_size = queries.shape[2]
     hidden = gate_weight.shape[1] // 2
 
-    halves = queries.reshape(4, 2, HEADS, head_size).transpose(1, 0, 2, 3)
-    sent = jnp.broadcast_to(halves[None], (CHIPS, *halves.shape)).reshape(32, 4, HEADS, head_size)
+    to_first = (jnp.arange(32) % 2 == 0)[:, None, None, None]
+    sent = jnp.where(to_first, queries[None, :, :HEADS], queries[None, :, HEADS:])
     core_only = core.reshape(1)
     shared = (mid_keys, mid_values, root_keys, root_values)
     sent, shared = lax.optimization_barrier((sent, shared))
@@ -449,7 +449,7 @@
     own = own_part(scalars, gathered, leaves)
     attended = merged(parts, *own)
     attended_near = exchange(attended, PLANE).reshape(128, HEADS * head_size)
-    pair, down_sent = cut(core_only, attended, gate_weight, up_weight, down_weight)
+    pair, down_sent = cut(core_only, gate_weight, up_weight, down_weight)
     attended_near, pair, down_sent = lax.optimization_barrier((attended_near, pair, down_sent))
     gain_far = swapped(norm_gain)
     attended_far, pair = lax.optimization_barrier((swapped(attended_near), pair))
@@ -472,14 +472,14 @@
     payload = gate_up(
         core_only, stream, stream_far, norm_gain[None], gain_far[None], gate_weight, up_weight, pair_far
     )
-    payload, down_sent = lax.optimization_barrier((payload, down_sent))
+    stream_rows = lax.dynamic_slice_in_dim(stream, lax.axis_index("mp") * 32, 32, 0)
+    payload, down_sent, stream_rows = lax.optimization_barrier((payload, down_sent, stream_rows))
     parts = exchange(payload.reshape(CHIPS, 8, -1), PLANE)
     own_down, far_down, token = load_down(core_only, down_weight, swapped(down_sent))
     acts = exchange(activation(parts, token), PLANE).reshape(128, hidden)
     blocks = down(core_only, acts, own_down, far_down).reshape(8, 32, -1)
     arrived = exchange(blocks, ("core", "mp"))
-    rows = lax.dynamic_slice_in_dim(stream, lax.axis_index("mp") * 32, 32, 0)
-    return (rows + jnp.sum(arrived.astype(f32), axis=0)).astype(bf16)
+    return (stream_rows + jnp.sum(arrived.astype(f32), axis=0)).astype(bf16)
 
 
 def solution(mesh):

time: 144 us -> 142 us (0.986)
  blocking collectives: 17.5 us -> 27.4 us
  starting transfers between devices: 39.5 us -> 33.8 us
  waiting for transfers between devices: 45.8 us -> 41 us
    all_to_all x1 -> x2, blocking collectives: 17.5 us -> 27.4 us  [exchange(): return lax.all_to_all(x, axes, split_axis=0, concat_axis=0, tiled=True)]
    all_to_all x5 -> x4, starting transfers between devices: 29.1 us -> 23.4 us  [exchange(): return lax.all_to_all(x, axes, split_axis=0, concat_axis=0, tiled=True)]
    all_to_all x5 -> x4, waiting for transfers between devices: 37 us -> 32.1 us  [exchange(): return lax.all_to_all(x, axes, split_axis=0, concat_axis=0, tiled=True)]
  transfers between devices with their start and end apart: 20 -> 19, of which waited for: 11 -> 10; matrix products, arithmetic and copies ran while one was open for 2% -> 2% of each run, Pallas kernels for 9% -> 9%
where the time goes in v3:
time: 142 us; the launch traced here: 141 us
  waiting for transfers between devices  41 us (29%)
  starting transfers between devices  33.8 us (24%)
  blocking collectives  27.4 us (19%)
  Pallas kernels  26.5 us (19%)
  local copies, waits for them, and re-layouts  8.37 us (6%)
  other arithmetic  3.36 us (2%)
    all_to_all x4, waiting for transfers between devices, exchange(): return lax.all_to_all(x, axes, split_axis=0, concat_axis=0, tiled=True)  32.1 us
    all_to_all x2, blocking collectives, exchange(): return lax.all_to_all(x, axes, split_axis=0, concat_axis=0, tiled=True)  27.4 us
    all_to_all x4, starting transfers between devices, exchange(): return lax.all_to_all(x, axes, split_axis=0, concat_axis=0, tiled=True)  23.4 us
    unnamed x38, local copies, waits for them, and re-layouts  6.59 us
    ppermute x12, starting transfers between devices, swapped(): return lax.ppermute(x, 'core', SWAP)  6.55 us
    pallas_call x1, Pallas kernels, shared_part(): pl.pallas_call(shared_kernel, out_shape=jax.ShapeDtypeStruct((CHIPS, 80,...  5.69 us
    pallas_call x1, Pallas kernels, gate_up(): pl.pallas_call(gate_up_kernel, out_shape=jax.ShapeDtypeStruct((128, 2 * h...  5.67 us
    ppermute x3, waiting for transfers between devices, on_device(): lax.ppermute(share, 'mp', [(i, (i + step) % 4) for i in range(4)])  5.63 us
  transfers between devices with their start and end apart: 19, of which 10 were waited for; matrix products, arithmetic and copies ran while one was open for 2% of the time, Pallas kernels for 9%

profile of v3, /device:TPU:1, one launch (start us, length us, event | category | flops | bytes accessed | tf_op | source)
XLA Modules:
  0.0 141.1 jit_solution(3005867251728446090)
XLA Ops:
  0.0 0.9 fusion.11
  0.9 0.8 broadcast_select_fusion
  1.7 9.4 %all-to-all-start = ((bf16[32,4,8,128]{3,2,1,0:T(8,128)(2,1)}), bf16[32,4,8,128]{3,2,1,0:T(8,128)(2,1)S(1)}, u32[]{:S(2)}, u32[]{:S(2)}) async-start(bf16[32,4,8,128]{3,2,1,0:T(8,128)(2,1)} %broadcast_select_fusion), calls=%async_computation | async-start | bytes 524288 | tf_op jit(solution)/shard_map/all_to_all | solution.py:24
  11.1 0.3 collective-permute-start
  11.5 0.3 collective-permute-start.1
  11.7 0.2 collective-permute-start.2
  12.0 0.3 collective-permute-start.3
  12.2 0.9 convert_reduce_fusion.1
  13.1 0.7 fusion.10
  13.8 0.1 iota_add_fusion
  13.9 0.1 fusion.9
  14.0 0.2 add.126.column_ref
  14.2 0.1 add.116.row_ref
  14.3 0.6 gather_fusion
  14.9 0.1 pad_add_fusion.scalars
  15.0 0.7 copy-done.7
  15.7 0.7 copy-done.9
  16.4 0.9 copy-done.5
  17.4 0.9 copy-done.6
  18.3 0.9 copy-done.8
  19.3 0.9 copy-done.10
  20.2 0.3 split_root.1.refs_4_
  20.6 0.0 copy-start.18
  20.6 5.7 %shared_part.1 = bf16[16,80,128]{2,1,0:T(8,128)(2,1)} custom-call(s32[3]{0:T(128)S(1)} %pad_add_fusion.scalars, bf16[1024,128]{1,0:T(8,128)(2,1)S(1)} %bitcast.38, s32[1024,1]{1,0:T(8,128)S(1)} %add.126.column_ref, s32[1,1024]{1,0:T(1,128)S(1)} %add.116.row_ref, bf16[2048,128]{1,0:T(8,128)(2,1)S(1)} %bitcast.40, bf16[2048,128]{1,0:T(8,128)(2,1)S(1)} %bitcast.41, ...), custom_call_target="tpu_custom_call" | custom-call | flops 800000000 | bytes 4300000 | tf_op jit(solution)/shard_map/shared_part/pallas_call | solution.py:176
  26.3 0.2 collective-permute-start.5
  26.5 0.3 collective-permute-start.6
  26.8 6.7 %all-to-all-start.1 = ((bf16[16,80,128]{2,1,0:T(8,128)(2,1)}), bf16[16,80,128]{2,1,0:T(8,128)(2,1)S(1)}, u32[]{:S(2)}, u32[]{:S(2)}) async-start(bf16[16,80,128]{2,1,0:T(8,128)(2,1)} %shared_part.1), calls=%async_computation.1 | async-start | bytes 655360 | tf_op jit(solution)/shard_map/all_to_all | solution.py:24
  33.5 0.7 collective-permute-start.4
  34.2 0.8 collective-permute-done.4
  35.1 0.1 pad_add_fusion.1.scalars
  35.1 3.2 %own_part.1 = (f32[64,128]{1,0:T(8,128)S(1)}, f32[64,128]{1,0:T(8,128)S(1)}, f32[64,128]{1,0:T(8,128)S(1)}) custom-call(s32[10]{0:T(128)S(1)} %pad_add_fusion.1.scalars, bf16[1024,128]{1,0:T(8,128)(2,1)S(1)} %bitcast.39, bf16[2048,128]{1,0:T(8,128)(2,1)} %bitcast.17.refs_0_, bf16[2048,128]{1,0:T(8,128)(2,1)} %bitcast.18.refs_1_, ...), custom_call_target="tpu_custom_call" | custom-call | flops 17000000 | bytes 400000 | tf_op jit(solution)/shard_map/own_part/pallas_call | solution.py:210
  38.4 4.0 %all-to-all-done.1.parts_ref = bf16[16,80,128]{2,1,0:T(8,128)(2,1)S(1)} async-done(((bf16[16,80,128]{2,1,0:T(8,128)(2,1)}), bf16[16,80,128]{2,1,0:T(8,128)(2,1)S(1)}, u32[]{:S(2)}, u32[]{:S(2)}) %all-to-all-start.1) | async-done | bytes 327712 | tf_op jit(solution)/shard_map/all_to_all | solution.py:24
  42.4 1.7 %merged.1 = bf16[16,8,1024]{2,1,0:T(8,128)(2,1)} custom-call(bf16[16,80,128]{2,1,0:T(8,128)(2,1)S(1)} %all-to-all-done.1.parts_ref, f32[64,128]{1,0:T(8,128)S(1)} %get-tuple-element.37.high_ref, f32[64,128]{1,0:T(8,128)S(1)} %get-tuple-element.38.total_ref, f32[64,128]{1,0:T(8,128)S(1)} %get-tuple-element.39.mean_ref), custom_call_target="tpu_custom_call" | custom-call | flops 4000000 | bytes 700000 | tf_op jit(solution)/shard_map/merged/pallas_call | solution.py:243
  44.0 3.5 %all-to-all-start.2 = ((bf16[16,8,1024]{2,1,0:T(8,128)(2,1)}), bf16[16,8,1024]{2,1,0:T(8,128)(2,1)S(1)}, u32[]{:S(2)}, u32[]{:S(2)}) async-start(bf16[16,8,1024]{2,1,0:T(8,128)(2,1)} %merged.1), calls=%async_computation.2 | async-start | bytes 524288 | tf_op jit(solution)/shard_map/all_to_all | solution.py:24
  47.6 5.1 %cut.1 = (bf16[512,3584]{1,0:T(8,128)(2,1)}, bf16[3584,256]{1,0:T(8,128)(2,1)}) custom-call(s32[1]{0:T(128)} %bitcast.core, bf16[256,7168]{1,0:T(8,128)(2,1)} %gate.3, bf16[256,7168]{1,0:T(8,128)(2,1)} %up.3, bf16[7168,256]{1,0:T(8,128)(2,1)} %weight.1), custom_call_target="tpu_custom_call" | custom-call | bytes 11000000 | tf_op jit(solution)/shard_map/cut/pallas_call | solution.py:67
  52.7 2.4 %all-to-all-done.2 = bf16[16,8,1024]{2,1,0:T(8,128)(2,1)S(1)} async-done(((bf16[16,8,1024]{2,1,0:T(8,128)(2,1)}), bf16[16,8,1024]{2,1,0:T(8,128)(2,1)S(1)}, u32[]{:S(2)}, u32[]{:S(2)}) %all-to-all-start.2) | async-done | bytes 262176 | tf_op jit(solution)/shard_map/all_to_all | solution.py:24
  55.1 2.7 %collective-permute-start.7 = (bf16[128,1024]{1,0:T(8,128)(2,1)S(1)}, bf16[128,1024]{1,0:T(8,128)(2,1)S(1)}, u32[]{:S(2)}, u32[]{:S(2)}) collective-permute-start(bf16[128,1024]{1,0:T(8,128)(2,1)S(1)} %bitcast.50), channel_id=1, source_target_pairs={{0,4},{4,0},{1,5},{5,1},{2,6},{6,2},{3,7},{7,3},{8,12},{12,8},{9,1... | collective-permute-start | bytes 786440 | tf_op jit(solution)/shard_map/ppermute | solution.py:28
  57.7 1.2 collective-permute-done.7
  58.9 0.4 collective-permute-start.13
  59.3 0.2 fusion.2
  59.5 0.2 fusion
  59.8 2.8 %collective-permute-start.10 = (bf16[128,256]{1,0:T(8,128)(2,1)S(1)}, bf16[128,256]{1,0:T(8,128)(2,1)S(1)}, u32[]{:S(2)}, u32[]{:S(2)}) collective-permute-start(bf16[128,256]{1,0:T(8,128)(2,1)S(1)} %fusion), channel_id=1, source_target_pairs={{0,3},{1,0},{2,1},{3,2},{4,7},{5,4},{6,5},{7,6},{8,11},{9,8},{10,9... | collective-permute-start | bytes 196616 | tf_op jit(solution)/shard_map/ppermute | solution.py:470
  62.6 0.3 collective-permute-start.9
  62.9 0.7 collective-permute-start.8
  63.6 0.3 collective-permute-done.10
  63.9 3.4 %collective-permute-done.9 = bf16[128,256]{1,0:T(8,128)(2,1)S(1)} collective-permute-done((bf16[128,256]{1,0:T(8,128)(2,1)S(1)}, bf16[128,256]{1,0:T(8,128)(2,1)S(1)}, u32[]{:S(2)}, u32[]{:S(2)}) %collective-permute-start.9) | collective-permute-done | bytes 65568 | tf_op jit(solution)/shard_map/ppermute | solution.py:470
  67.3 2.0 %collective-permute-done.8 = bf16[128,256]{1,0:T(8,128)(2,1)S(1)} collective-permute-done((bf16[128,256]{1,0:T(8,128)(2,1)S(1)}, bf16[128,256]{1,0:T(8,128)(2,1)S(1)}, u32[]{:S(2)}, u32[]{:S(2)}) %collective-permute-start.8) | collective-permute-done | bytes 65568 | tf_op jit(solution)/shard_map/ppermute | solution.py:470
  69.3 0.8 collective-permute-start.11
  70.1 0.1 collective-permute-start.12
  70.2 1.0 collective-permute-done.12
  71.3 0.5 copy-done.17
  71.8 0.1 copy-done.14
  71.9 5.7 %gate_up.1 = bf16[128,7296]{1,0:T(8,128)(2,1)} custom-call(s32[1]{0:T(128)} %bitcast.core, f32[128,256]{1,0:T(8,128)} %copy-done.13, f32[128,256]{1,0:T(8,128)} %copy-done.14, f32[1,256]{1,0:T(1,128)} %bitcast.52, f32[1,256]{1,0:T(1,128)} %bitcast.53, bf16[256,7168]{1,0:T(8,128)(2,1)} %gate.3, bf16[256,7168]{1,0:T(8,128)(2,1)} %up.3, ...), custom_call_target="tpu_custom_call" | custom-call | flops 940000000 | bytes 9400000 | tf_op jit(solution)/shard_map/gate_up/pallas_call | solution.py:300
  77.6 0.3 collective-permute-start.14
  77.9 3.7 %all-to-all-start.3 = ((bf16[16,8,7296]{2,1,0:T(8,128)(2,1)}), bf16[16,8,7296]{2,1,0:T(8,128)(2,1)S(1)}, u32[]{:S(2)}, u32[]{:S(2)}) async-start(bf16[16,8,7296]{2,1,0:T(8,128)(2,1)} %bitcast.49), calls=%async_computation.3 | async-start | bytes 3735552 | tf_op jit(solution)/shard_map/all_to_all | solution.py:24
  81.6 0.2 collective-permute-done.14.far_ref
  81.8 3.9 %load_down.1 = (bf16[3584,256]{1,0:T(8,128)(2,1)}, bf16[3584,256]{1,0:T(8,128)(2,1)}, f32[8,128]{1,0:T(8,128)}) custom-call(s32[1]{0:T(128)} %bitcast.core, bf16[7168,256]{1,0:T(8,128)(2,1)} %weight.1, bf16[3584,256]{1,0:T(8,128)(2,1)} %collective-permute-done.14.far_ref), custom_call_target="tpu_custom_call" | custom-call | bytes 7400000 | tf_op jit(solution)/shard_map/load_down/pallas_call | solution.py:333
  85.7 25.7 %all-to-all-done.3.parts_ref = bf16[16,8,7296]{2,1,0:T(8,128)(2,1)S(1)} async-done(((bf16[16,8,7296]{2,1,0:T(8,128)(2,1)}), bf16[16,8,7296]{2,1,0:T(8,128)(2,1)S(1)}, u32[]{:S(2)}, u32[]{:S(2)}) %all-to-all-start.3) | async-done | bytes 1867808 | tf_op jit(solution)/shard_map/all_to_all | solution.py:24
  111.4 0.7 copy-done.11
  112.1 0.3 activation.1
  112.4 17.5 %all_to_all.30 = bf16[16,8,3584]{2,1,0:T(8,128)(2,1)S(1)} all-to-all(bf16[16,8,3584]{2,1,0:T(8,128)(2,1)S(1)} %activation.1), channel_id=1, replica_groups=mesh['z'=4,'x'=4,'core'=2,'mp'=4] {'z','x'}, dimensions={0} | all-to-all | bytes 1835008 | tf_op jit(solution)/shard_map/all_to_all | solution.py:24
  129.9 0.7 down.3
  130.6 9.9 %all_to_all.31 = bf16[8,32,256]{2,1,0:T(8,128)(2,1)S(1)} all-to-all(bf16[8,32,256]{2,1,0:T(8,128)(2,1)S(1)} %bitcast.44), channel_id=1, replica_groups=mesh['z'=4,'x'=4,'core'=2,'mp'=4] {'core','mp'}, dimensions={0} | all-to-all | bytes 262144 | tf_op jit(solution)/shard_map/all_to_all | solution.py:24
  140.5 0.6 add_convert_fusion
  (42 shorter events, 0.2 us)
Async XLA Ops:
  0.0 59.3 %copy-start = (bf16[2048,256]{1,0:T(8,128)(2,1)S(1)}, bf16[2048,256]{1,0:T(8,128)(2,1)}, u32[]{:S(2)}) copy-start(bf16[2048,256]{1,0:T(8,128)(2,1)} %param.28) | copy-start | bytes 3145732
  0.0 20.6 %copy-start.3 = (bf16[1,1024,2,128]{3,2,1,0:T(2,128)(2,1)S(1)}, bf16[1,1024,2,128]{3,2,1,0:T(2,128)(2,1)}, u32[]{:S(2)}) copy-start(bf16[1,1024,2,128]{3,2,1,0:T(2,128)(2,1)} %param.19) | copy-start | bytes 1572868
  0.0 20.6 %copy-start.4 = (bf16[1,1024,2,128]{3,2,1,0:T(2,128)(2,1)S(1)}, bf16[1,1024,2,128]{3,2,1,0:T(2,128)(2,1)}, u32[]{:S(2)}) copy-start(bf16[1,1024,2,128]{3,2,1,0:T(2,128)(2,1)} %param.20) | copy-start | bytes 1572868
  0.0 14.3 %copy-start.12 = (s32[32]{0:T(128)S(1)}, s32[32]{0:T(128)}, u32[]{:S(2)}) copy-start(s32[32]{0:T(128)} %param.23) | copy-start | bytes 388
  1.7 18.9 %all-to-all-start = ((bf16[32,4,8,128]{3,2,1,0:T(8,128)(2,1)}), bf16[32,4,8,128]{3,2,1,0:T(8,128)(2,1)S(1)}, u32[]{:S(2)}, u32[]{:S(2)}) async-start(bf16[32,4,8,128]{3,2,1,0:T(8,128)(2,1)} %broadcast_select_fusion), calls=%async_computation | async-start | bytes 524288 | tf_op jit(solution)/shard_map/all_to_all | solution.py:24
  11.1 9.4 %collective-permute-start = (bf16[1,1024,2,128]{3,2,1,0:T(2,128)(2,1)}, bf16[1,1024,2,128]{3,2,1,0:T(2,128)(2,1)}, u32[]{:S(2)}, u32[]{:S(2)}) collective-permute-start(bf16[1,1024,2,128]{3,2,1,0:T(2,128)(2,1)} %param.19), channel_id=1, source_target_pairs={{0,4},{4,0},{1,5},{5,1},{2,6},{6,2},{3,7},{7,3},{8,12},{12,8},{9,1... | collective-permute-start | bytes 1572872 | tf_op jit(solution)/shard_map/ppermute | solution.py:28
  11.5 9.1 %collective-permute-start.1 = (bf16[1,1024,2,128]{3,2,1,0:T(2,128)(2,1)}, bf16[1,1024,2,128]{3,2,1,0:T(2,128)(2,1)}, u32[]{:S(2)}, u32[]{:S(2)}) collective-permute-start(bf16[1,1024,2,128]{3,2,1,0:T(2,128)(2,1)} %param.20), channel_id=1, source_target_pairs={{0,4},{4,0},{1,5},{5,1},{2,6},{6,2},{3,7},{7,3},{8,12},{12,8},{9,1... | collective-permute-start | bytes 1572872 | tf_op jit(solution)/shard_map/ppermute | solution.py:28
  11.7 3.3 %collective-permute-start.2 = (bf16[512,2,128]{2,1,0:T(2,128)(2,1)}, bf16[512,2,128]{2,1,0:T(2,128)(2,1)S(1)}, u32[]{:S(2)}, u32[]{:S(2)}) collective-permute-start(bf16[512,2,128]{2,1,0:T(2,128)(2,1)} %param.17), channel_id=1, source_target_pairs={{0,4},{4,0},{1,5},{5,1},{2,6},{6,2},{3,7},{7,3},{8,12},{12,8},{9,1... | collective-permute-start | bytes 786440 | tf_op jit(solution)/shard_map/ppermute | solution.py:28
  12.0 3.8 %collective-permute-start.3 = (bf16[512,2,128]{2,1,0:T(2,128)(2,1)}, bf16[512,2,128]{2,1,0:T(2,128)(2,1)S(1)}, u32[]{:S(2)}, u32[]{:S(2)}) collective-permute-start(bf16[512,2,128]{2,1,0:T(2,128)(2,1)} %param.18), channel_id=1, source_target_pairs={{0,4},{4,0},{1,5},{5,1},{2,6},{6,2},{3,7},{7,3},{8,12},{12,8},{9,1... | collective-permute-start | bytes 786440 | tf_op jit(solution)/shard_map/ppermute | solution.py:28
  15.0 0.7 copy-start.7
  15.7 0.7 copy-start.9
  16.4 0.9 copy-start.5
  17.4 0.9 copy-start.6
  18.3 0.9 copy-start.8
  19.3 0.9 copy-start.10
  20.6 12.9 %copy-start.18 = (s32[4]{0:T(128)S(1)}, s32[4]{0:T(128)}, u32[]{:S(2)}) copy-start(s32[4]{0:T(128)} %param.24) | copy-start | bytes 52
  26.3 8.8 %collective-permute-start.5 = (bf16[4,256,2,128]{3,2,1,0:T(2,128)(2,1)}, bf16[4,256,2,128]{3,2,1,0:T(2,128)(2,1)S(1)}, u32[]{:S(2)}, u32[]{:S(2)}) collective-permute-start(bf16[4,256,2,128]{3,2,1,0:T(2,128)(2,1)} %param.21), channel_id=1, source_target_pairs={{0,4},{4,0},{1,5},{5,1},{2,6},{6,2},{3,7},{7,3},{8,12},{12,8},{9,1... | collective-permute-start | bytes 1572872 | tf_op jit(solution)/shard_map/ppermute | solution.py:28
  26.5 8.6 %collective-permute-start.6 = (bf16[4,256,2,128]{3,2,1,0:T(2,128)(2,1)}, bf16[4,256,2,128]{3,2,1,0:T(2,128)(2,1)S(1)}, u32[]{:S(2)}, u32[]{:S(2)}) collective-permute-start(bf16[4,256,2,128]{3,2,1,0:T(2,128)(2,1)} %param.22), channel_id=1, source_target_pairs={{0,4},{4,0},{1,5},{5,1},{2,6},{6,2},{3,7},{7,3},{8,12},{12,8},{9,1... | collective-permute-start | bytes 1572872 | tf_op jit(solution)/shard_map/ppermute | solution.py:28
  26.8 15.5 %all-to-all-start.1 = ((bf16[16,80,128]{2,1,0:T(8,128)(2,1)}), bf16[16,80,128]{2,1,0:T(8,128)(2,1)S(1)}, u32[]{:S(2)}, u32[]{:S(2)}) async-start(bf16[16,80,128]{2,1,0:T(8,128)(2,1)} %shared_part.1), calls=%async_computation.1 | async-start | bytes 655360 | tf_op jit(solution)/shard_map/all_to_all | solution.py:24
  33.5 1.5 %collective-permute-start.4 = (s32[4]{0:T(128)S(1)}, s32[4]{0:T(128)S(1)}, u32[]{:S(2)}, u32[]{:S(2)}) collective-permute-start(s32[4]{0:T(128)S(1)} %copy-done.18), channel_id=1, source_target_pairs={{0,4},{4,0},{1,5},{5,1},{2,6},{6,2},{3,7},{7,3},{8,12},{12,8},{9,1... | collective-permute-start | bytes 56 | tf_op jit(solution)/shard_map/ppermute | solution.py:28
  44.0 11.0 %all-to-all-start.2 = ((bf16[16,8,1024]{2,1,0:T(8,128)(2,1)}), bf16[16,8,1024]{2,1,0:T(8,128)(2,1)S(1)}, u32[]{:S(2)}, u32[]{:S(2)}) async-start(bf16[16,8,1024]{2,1,0:T(8,128)(2,1)} %merged.1), calls=%async_computation.2 | async-start | bytes 524288 | tf_op jit(solution)/shard_map/all_to_all | solution.py:24
  52.7 16.6 %copy-start.15 = (bf16[128,256]{1,0:T(8,128)(2,1)S(1)}, bf16[128,256]{1,0:T(8,128)(2,1)}, u32[]{:S(2)}) copy-start(bf16[128,256]{1,0:T(8,128)(2,1)} %param.26) | copy-start | bytes 196612
  52.7 17.4 %copy-start.16 = (f32[256]{0:T(256)S(1)}, f32[256]{0:T(256)}, u32[]{:S(2)}) copy-start(f32[256]{0:T(256)} %param.27) | copy-start | bytes 3076
  55.1 3.8 %collective-permute-start.7 = (bf16[128,1024]{1,0:T(8,128)(2,1)S(1)}, bf16[128,1024]{1,0:T(8,128)(2,1)S(1)}, u32[]{:S(2)}, u32[]{:S(2)}) collective-permute-start(bf16[128,1024]{1,0:T(8,128)(2,1)S(1)} %bitcast.50), channel_id=1, source_target_pairs={{0,4},{4,0},{1,5},{5,1},{2,6},{6,2},{3,7},{7,3},{8,12},{12,8},{9,1... | collective-permute-start | bytes 786440 | tf_op jit(solution)/shard_map/ppermute | solution.py:28
  58.9 12.4 %collective-permute-start.13 = (bf16[512,3584]{1,0:T(8,128)(2,1)}, bf16[512,3584]{1,0:T(8,128)(2,1)}, u32[]{:S(2)}, u32[]{:S(2)}) collective-permute-start(bf16[512,3584]{1,0:T(8,128)(2,1)} %get-tuple-element.45), channel_id=1, source_target_pairs={{0,4},{4,0},{1,5},{5,1},{2,6},{6,2},{3,7},{7,3},{8,12},{12,8},{9,1... | collective-permute-start | bytes 11010056 | tf_op jit(solution)/shard_map/ppermute | solution.py:28
  59.8 4.1 %collective-permute-start.10 = (bf16[128,256]{1,0:T(8,128)(2,1)S(1)}, bf16[128,256]{1,0:T(8,128)(2,1)S(1)}, u32[]{:S(2)}, u32[]{:S(2)}) collective-permute-start(bf16[128,256]{1,0:T(8,128)(2,1)S(1)} %fusion), channel_id=1, source_target_pairs={{0,3},{1,0},{2,1},{3,2},{4,7},{5,4},{6,5},{7,6},{8,11},{9,8},{10,9... | collective-permute-start | bytes 196616 | tf_op jit(solution)/shard_map/ppermute | solution.py:470
  62.6 4.7 %collective-permute-start.9 = (bf16[128,256]{1,0:T(8,128)(2,1)S(1)}, bf16[128,256]{1,0:T(8,128)(2,1)S(1)}, u32[]{:S(2)}, u32[]{:S(2)}) collective-permute-start(bf16[128,256]{1,0:T(8,128)(2,1)S(1)} %fusion), channel_id=1, source_target_pairs={{0,2},{1,3},{2,0},{3,1},{4,6},{5,7},{6,4},{7,5},{8,10},{9,11},{10,... | collective-permute-start | bytes 196616 | tf_op jit(solution)/shard_map/ppermute | solution.py:470
  62.9 6.3 %collective-permute-start.8 = (bf16[128,256]{1,0:T(8,128)(2,1)S(1)}, bf16[128,256]{1,0:T(8,128)(2,1)S(1)}, u32[]{:S(2)}, u32[]{:S(2)}) collective-permute-start(bf16[128,256]{1,0:T(8,128)(2,1)S(1)} %fusion), channel_id=1, source_target_pairs={{0,1},{1,2},{2,3},{3,0},{4,5},{5,6},{6,7},{7,4},{8,9},{9,10},{10,1... | collective-permute-start | bytes 196616 | tf_op jit(solution)/shard_map/ppermute | solution.py:470
  69.3 2.0 %copy-start.13 = (f32[128,256]{1,0:T(8,128)}, f32[128,256]{1,0:T(8,128)S(1)}, u32[]{:S(2)}) copy-start(f32[128,256]{1,0:T(8,128)S(1)} %convert_add_fusion.near_ref) | copy-start | bytes 393220
  69.3 2.0 %collective-permute-start.11 = (f32[128,256]{1,0:T(8,128)S(1)}, f32[128,256]{1,0:T(8,128)S(1)}, u32[]{:S(2)}, u32[]{:S(2)}) collective-permute-start(f32[128,256]{1,0:T(8,128)S(1)} %convert_add_fusion.near_ref), channel_id=1, source_target_pairs={{0,4},{4,0},{1,5},{5,1},{2,6},{6,2},{3,7},{7,3},{8,12},{12,8},{9,1... | collective-permute-start | bytes 393224 | tf_op jit(solution)/shard_map/ppermute | solution.py:28
  70.1 1.1 collective-permute-start.12
  71.3 0.6 copy-start.17
  71.3 0.7 copy-start.14
  77.6 4.2 %collective-permute-start.14 = (bf16[3584,256]{1,0:T(8,128)(2,1)}, bf16[3584,256]{1,0:T(8,128)(2,1)}, u32[]{:S(2)}, u32[]{:S(2)}) collective-permute-start(bf16[3584,256]{1,0:T(8,128)(2,1)} %get-tuple-element.49), channel_id=1, source_target_pairs={{0,4},{4,0},{1,5},{5,1},{2,6},{6,2},{3,7},{7,3},{8,12},{12,8},{9,1... | collective-permute-start | bytes 5505032 | tf_op jit(solution)/shard_map/ppermute | solution.py:28
  77.9 33.6 %all-to-all-start.3 = ((bf16[16,8,7296]{2,1,0:T(8,128)(2,1)}), bf16[16,8,7296]{2,1,0:T(8,128)(2,1)S(1)}, u32[]{:S(2)}, u32[]{:S(2)}) async-start(bf16[16,8,7296]{2,1,0:T(8,128)(2,1)} %bitcast.49), calls=%async_computation.3 | async-start | bytes 3735552 | tf_op jit(solution)/shard_map/all_to_all | solution.py:24
  111.4 0.7 copy-start.11
  112.1 17.8 %copy-start.1 = (bf16[3584,256]{1,0:T(8,128)(2,1)S(1)}, bf16[3584,256]{1,0:T(8,128)(2,1)}, u32[]{:S(2)}) copy-start(bf16[3584,256]{1,0:T(8,128)(2,1)} %get-tuple-element.51.near) | copy-start | bytes 5505028
  112.1 17.8 %copy-start.2 = (bf16[3584,256]{1,0:T(8,128)(2,1)S(1)}, bf16[3584,256]{1,0:T(8,128)(2,1)}, u32[]{:S(2)}) copy-start(bf16[3584,256]{1,0:T(8,128)(2,1)} %get-tuple-element.52.far) | copy-start | bytes 5505028

commit v4 on v3

--- a/solution.py
+++ b/solution.py
@@ -128,7 +128,7 @@
     level_row = jnp.sum(jnp.where(eye, level, 0.0), axis=0, keepdims=True)
     first = mean.astype(bf16)
     second = (mean - first.astype(f32)).astype(bf16)
-    step = 256
+    step = 512
     lanes = iota((64, 128), 1)
     diagonal = (lanes % 64) == iota((64, 128), 0)
     for at in range(0, count, step):
@@ -251,7 +251,7 @@
     )(parts, high, total, mean)
 
 
-TILE = 1792
+TILE = 896
 
 
 def gate_up_kernel(core, near_ref, far_ref, gain_ref, far_gain_ref, gate, up, pair, out, held, scaled, result, sems, out_sems):

time: 142 us -> 141 us (level)
  no operation moved by 1% of the time
where the time goes in v4:
time: 141 us
  waiting for transfers between devices  40.9 us (29%)
  starting transfers between devices  33.8 us (24%)
  blocking collectives  27.4 us (19%)
  Pallas kernels  26 us (18%)
  local copies, waits for them, and re-layouts  8.37 us (6%)
  other arithmetic  3.36 us (2%)
    all_to_all x4, waiting for transfers between devices, exchange(): return lax.all_to_all(x, axes, split_axis=0, concat_axis=0, tiled=True)  32.1 us
    all_to_all x2, blocking collectives, exchange(): return lax.all_to_all(x, axes, split_axis=0, concat_axis=0, tiled=True)  27.4 us
    all_to_all x4, starting transfers between devices, exchange(): return lax.all_to_all(x, axes, split_axis=0, concat_axis=0, tiled=True)  23.4 us
    unnamed x38, local copies, waits for them, and re-layouts  6.59 us
    ppermute x12, starting transfers between devices, swapped(): return lax.ppermute(x, 'core', SWAP)  6.58 us
    pallas_call x1, Pallas kernels, gate_up(): pl.pallas_call(gate_up_kernel, out_shape=jax.ShapeDtypeStruct((128, 2 * h...  5.67 us
    ppermute x3, waiting for transfers between devices, on_device(): lax.ppermute(share, 'mp', [(i, (i + step) % 4) for i in range(4)])  5.61 us
    pallas_call x1, Pallas kernels, shared_part(): pl.pallas_call(shared_kernel, out_shape=jax.ShapeDtypeStruct((CHIPS, 80,...  5.18 us
  transfers between devices with their start and end apart: 19, of which 10 were waited for; matrix products, arithmetic and copies ran while one was open for 2% of the time, Pallas kernels for 9%

profile of v4, /device:TPU:1, one launch (start us, length us, event | category | flops | bytes accessed | tf_op | source)
XLA Modules:
  0.0 140.6 jit_solution(14221197886911750221)
XLA Ops:
  0.0 0.9 fusion.11
  0.9 0.8 broadcast_select_fusion
  1.7 9.4 %all-to-all-start = ((bf16[32,4,8,128]{3,2,1,0:T(8,128)(2,1)}), bf16[32,4,8,128]{3,2,1,0:T(8,128)(2,1)S(1)}, u32[]{:S(2)}, u32[]{:S(2)}) async-start(bf16[32,4,8,128]{3,2,1,0:T(8,128)(2,1)} %broadcast_select_fusion), calls=%async_computation | async-start | bytes 524288 | tf_op jit(solution)/shard_map/all_to_all | solution.py:24
  11.1 0.3 collective-permute-start
  11.5 0.3 collective-permute-start.1
  11.7 0.2 collective-permute-start.2
  12.0 0.3 collective-permute-start.3
  12.2 0.9 convert_reduce_fusion.1
  13.1 0.7 fusion.10
  13.8 0.1 iota_add_fusion
  13.9 0.1 fusion.9
  14.0 0.2 add.126.column_ref
  14.2 0.1 add.116.row_ref
  14.3 0.6 gather_fusion
  14.9 0.1 pad_add_fusion.scalars
  15.0 0.7 copy-done.7
  15.7 0.7 copy-done.9
  16.4 0.9 copy-done.5
  17.4 0.9 copy-done.6
  18.3 0.9 copy-done.8
  19.3 0.9 copy-done.10
  20.2 0.3 split_root.1.refs_4_
  20.6 0.0 copy-start.18
  20.6 5.2 %shared_part.1 = bf16[16,80,128]{2,1,0:T(8,128)(2,1)} custom-call(s32[3]{0:T(128)S(1)} %pad_add_fusion.scalars, bf16[1024,128]{1,0:T(8,128)(2,1)S(1)} %bitcast.38, s32[1024,1]{1,0:T(8,128)S(1)} %add.126.column_ref, s32[1,1024]{1,0:T(1,128)S(1)} %add.116.row_ref, bf16[2048,128]{1,0:T(8,128)(2,1)S(1)} %bitcast.40, bf16[2048,128]{1,0:T(8,128)(2,1)S(1)} %bitcast.41, ...), custom_call_target="tpu_custom_call" | custom-call | flops 800000000 | bytes 4300000 | tf_op jit(solution)/shard_map/shared_part/pallas_call | solution.py:176
  25.8 0.2 collective-permute-start.5
  26.0 0.3 collective-permute-start.6
  26.3 6.7 %all-to-all-start.1 = ((bf16[16,80,128]{2,1,0:T(8,128)(2,1)}), bf16[16,80,128]{2,1,0:T(8,128)(2,1)S(1)}, u32[]{:S(2)}, u32[]{:S(2)}) async-start(bf16[16,80,128]{2,1,0:T(8,128)(2,1)} %shared_part.1), calls=%async_computation.1 | async-start | bytes 655360 | tf_op jit(solution)/shard_map/all_to_all | solution.py:24
  33.0 0.7 collective-permute-start.4
  33.7 0.8 collective-permute-done.4
  34.6 0.1 pad_add_fusion.1.scalars
  34.6 3.2 %own_part.1 = (f32[64,128]{1,0:T(8,128)S(1)}, f32[64,128]{1,0:T(8,128)S(1)}, f32[64,128]{1,0:T(8,128)S(1)}) custom-call(s32[10]{0:T(128)S(1)} %pad_add_fusion.1.scalars, bf16[1024,128]{1,0:T(8,128)(2,1)S(1)} %bitcast.39, bf16[2048,128]{1,0:T(8,128)(2,1)} %bitcast.17.refs_0_, bf16[2048,128]{1,0:T(8,128)(2,1)} %bitcast.18.refs_1_, ...), custom_call_target="tpu_custom_call" | custom-call | flops 17000000 | bytes 400000 | tf_op jit(solution)/shard_map/own_part/pallas_call | solution.py:210
  37.8 4.0 %all-to-all-done.1.parts_ref = bf16[16,80,128]{2,1,0:T(8,128)(2,1)S(1)} async-done(((bf16[16,80,128]{2,1,0:T(8,128)(2,1)}), bf16[16,80,128]{2,1,0:T(8,128)(2,1)S(1)}, u32[]{:S(2)}, u32[]{:S(2)}) %all-to-all-start.1) | async-done | bytes 327712 | tf_op jit(solution)/shard_map/all_to_all | solution.py:24
  41.8 1.7 %merged.1 = bf16[16,8,1024]{2,1,0:T(8,128)(2,1)} custom-call(bf16[16,80,128]{2,1,0:T(8,128)(2,1)S(1)} %all-to-all-done.1.parts_ref, f32[64,128]{1,0:T(8,128)S(1)} %get-tuple-element.37.high_ref, f32[64,128]{1,0:T(8,128)S(1)} %get-tuple-element.38.total_ref, f32[64,128]{1,0:T(8,128)S(1)} %get-tuple-element.39.mean_ref), custom_call_target="tpu_custom_call" | custom-call | flops 4000000 | bytes 700000 | tf_op jit(solution)/shard_map/merged/pallas_call | solution.py:243
  43.5 3.5 %all-to-all-start.2 = ((bf16[16,8,1024]{2,1,0:T(8,128)(2,1)}), bf16[16,8,1024]{2,1,0:T(8,128)(2,1)S(1)}, u32[]{:S(2)}, u32[]{:S(2)}) async-start(bf16[16,8,1024]{2,1,0:T(8,128)(2,1)} %merged.1), calls=%async_computation.2 | async-start | bytes 524288 | tf_op jit(solution)/shard_map/all_to_all | solution.py:24
  47.0 5.1 %cut.1 = (bf16[512,3584]{1,0:T(8,128)(2,1)}, bf16[3584,256]{1,0:T(8,128)(2,1)}) custom-call(s32[1]{0:T(128)} %bitcast.core, bf16[256,7168]{1,0:T(8,128)(2,1)} %gate.3, bf16[256,7168]{1,0:T(8,128)(2,1)} %up.3, bf16[7168,256]{1,0:T(8,128)(2,1)} %weight.1), custom_call_target="tpu_custom_call" | custom-call | bytes 11000000 | tf_op jit(solution)/shard_map/cut/pallas_call | solution.py:67
  52.2 2.4 %all-to-all-done.2 = bf16[16,8,1024]{2,1,0:T(8,128)(2,1)S(1)} async-done(((bf16[16,8,1024]{2,1,0:T(8,128)(2,1)}), bf16[16,8,1024]{2,1,0:T(8,128)(2,1)S(1)}, u32[]{:S(2)}, u32[]{:S(2)}) %all-to-all-start.2) | async-done | bytes 262176 | tf_op jit(solution)/shard_map/all_to_all | solution.py:24
  54.6 2.7 %collective-permute-start.7 = (bf16[128,1024]{1,0:T(8,128)(2,1)S(1)}, bf16[128,1024]{1,0:T(8,128)(2,1)S(1)}, u32[]{:S(2)}, u32[]{:S(2)}) collective-permute-start(bf16[128,1024]{1,0:T(8,128)(2,1)S(1)} %bitcast.50), channel_id=1, source_target_pairs={{0,4},{4,0},{1,5},{5,1},{2,6},{6,2},{3,7},{7,3},{8,12},{12,8},{9,1... | collective-permute-start | bytes 786440 | tf_op jit(solution)/shard_map/ppermute | solution.py:28
  57.2 1.2 collective-permute-done.7
  58.4 0.4 collective-permute-start.13
  58.7 0.2 fusion.2
  59.0 0.3 fusion
  59.3 2.8 %collective-permute-start.10 = (bf16[128,256]{1,0:T(8,128)(2,1)S(1)}, bf16[128,256]{1,0:T(8,128)(2,1)S(1)}, u32[]{:S(2)}, u32[]{:S(2)}) collective-permute-start(bf16[128,256]{1,0:T(8,128)(2,1)S(1)} %fusion), channel_id=1, source_target_pairs={{0,3},{1,0},{2,1},{3,2},{4,7},{5,4},{6,5},{7,6},{8,11},{9,8},{10,9... | collective-permute-start | bytes 196616 | tf_op jit(solution)/shard_map/ppermute | solution.py:470
  62.0 0.3 collective-permute-start.9
  62.4 0.7 collective-permute-start.8
  63.1 0.3 collective-permute-done.10
  63.4 3.4 %collective-permute-done.9 = bf16[128,256]{1,0:T(8,128)(2,1)S(1)} collective-permute-done((bf16[128,256]{1,0:T(8,128)(2,1)S(1)}, bf16[128,256]{1,0:T(8,128)(2,1)S(1)}, u32[]{:S(2)}, u32[]{:S(2)}) %collective-permute-start.9) | collective-permute-done | bytes 65568 | tf_op jit(solution)/shard_map/ppermute | solution.py:470
  66.7 2.0 %collective-permute-done.8 = bf16[128,256]{1,0:T(8,128)(2,1)S(1)} collective-permute-done((bf16[128,256]{1,0:T(8,128)(2,1)S(1)}, bf16[128,256]{1,0:T(8,128)(2,1)S(1)}, u32[]{:S(2)}, u32[]{:S(2)}) %collective-permute-start.8) | collective-permute-done | bytes 65568 | tf_op jit(solution)/shard_map/ppermute | solution.py:470
  68.8 0.8 collective-permute-start.11
  69.6 0.1 collective-permute-start.12
  69.7 1.0 collective-permute-done.12
  70.8 0.5 copy-done.17
  71.3 0.1 copy-done.14
  71.4 5.7 %gate_up.1 = bf16[128,7296]{1,0:T(8,128)(2,1)} custom-call(s32[1]{0:T(128)} %bitcast.core, f32[128,256]{1,0:T(8,128)} %copy-done.13, f32[128,256]{1,0:T(8,128)} %copy-done.14, f32[1,256]{1,0:T(1,128)} %bitcast.52, f32[1,256]{1,0:T(1,128)} %bitcast.53, bf16[256,7168]{1,0:T(8,128)(2,1)} %gate.3, bf16[256,7168]{1,0:T(8,128)(2,1)} %up.3, ...), custom_call_target="tpu_custom_call" | custom-call | flops 940000000 | bytes 9400000 | tf_op jit(solution)/shard_map/gate_up/pallas_call | solution.py:300
  77.1 0.3 collective-permute-start.14
  77.4 3.7 %all-to-all-start.3 = ((bf16[16,8,7296]{2,1,0:T(8,128)(2,1)}), bf16[16,8,7296]{2,1,0:T(8,128)(2,1)S(1)}, u32[]{:S(2)}, u32[]{:S(2)}) async-start(bf16[16,8,7296]{2,1,0:T(8,128)(2,1)} %bitcast.49), calls=%async_computation.3 | async-start | bytes 3735552 | tf_op jit(solution)/shard_map/all_to_all | solution.py:24
  81.1 0.2 collective-permute-done.14.far_ref
  81.3 3.9 %load_down.1 = (bf16[3584,256]{1,0:T(8,128)(2,1)}, bf16[3584,256]{1,0:T(8,128)(2,1)}, f32[8,128]{1,0:T(8,128)}) custom-call(s32[1]{0:T(128)} %bitcast.core, bf16[7168,256]{1,0:T(8,128)(2,1)} %weight.1, bf16[3584,256]{1,0:T(8,128)(2,1)} %collective-permute-done.14.far_ref), custom_call_target="tpu_custom_call" | custom-call | bytes 7400000 | tf_op jit(solution)/shard_map/load_down/pallas_call | solution.py:333
  85.2 25.7 %all-to-all-done.3.parts_ref = bf16[16,8,7296]{2,1,0:T(8,128)(2,1)S(1)} async-done(((bf16[16,8,7296]{2,1,0:T(8,128)(2,1)}), bf16[16,8,7296]{2,1,0:T(8,128)(2,1)S(1)}, u32[]{:S(2)}, u32[]{:S(2)}) %all-to-all-start.3) | async-done | bytes 1867808 | tf_op jit(solution)/shard_map/all_to_all | solution.py:24
  110.9 0.7 copy-done.11
  111.6 0.3 activation.1
  111.9 17.5 %all_to_all.30 = bf16[16,8,3584]{2,1,0:T(8,128)(2,1)S(1)} all-to-all(bf16[16,8,3584]{2,1,0:T(8,128)(2,1)S(1)} %activation.1), channel_id=1, replica_groups=mesh['z'=4,'x'=4,'core'=2,'mp'=4] {'z','x'}, dimensions={0} | all-to-all | bytes 1835008 | tf_op jit(solution)/shard_map/all_to_all | solution.py:24
  129.4 0.6 down.3
  130.0 9.9 %all_to_all.31 = bf16[8,32,256]{2,1,0:T(8,128)(2,1)S(1)} all-to-all(bf16[8,32,256]{2,1,0:T(8,128)(2,1)S(1)} %bitcast.44), channel_id=1, replica_groups=mesh['z'=4,'x'=4,'core'=2,'mp'=4] {'core','mp'}, dimensions={0} | all-to-all | bytes 262144 | tf_op jit(solution)/shard_map/all_to_all | solution.py:24
  140.0 0.6 add_convert_fusion
  (42 shorter events, 0.2 us)
Async XLA Ops:
  0.0 58.7 %copy-start = (bf16[2048,256]{1,0:T(8,128)(2,1)S(1)}, bf16[2048,256]{1,0:T(8,128)(2,1)}, u32[]{:S(2)}) copy-start(bf16[2048,256]{1,0:T(8,128)(2,1)} %param.28) | copy-start | bytes 3145732
  0.0 20.6 %copy-start.3 = (bf16[1,1024,2,128]{3,2,1,0:T(2,128)(2,1)S(1)}, bf16[1,1024,2,128]{3,2,1,0:T(2,128)(2,1)}, u32[]{:S(2)}) copy-start(bf16[1,1024,2,128]{3,2,1,0:T(2,128)(2,1)} %param.19) | copy-start | bytes 1572868
  0.0 20.6 %copy-start.4 = (bf16[1,1024,2,128]{3,2,1,0:T(2,128)(2,1)S(1)}, bf16[1,1024,2,128]{3,2,1,0:T(2,128)(2,1)}, u32[]{:S(2)}) copy-start(bf16[1,1024,2,128]{3,2,1,0:T(2,128)(2,1)} %param.20) | copy-start | bytes 1572868
  0.0 14.3 %copy-start.12 = (s32[32]{0:T(128)S(1)}, s32[32]{0:T(128)}, u32[]{:S(2)}) copy-start(s32[32]{0:T(128)} %param.23) | copy-start | bytes 388
  1.7 18.9 %all-to-all-start = ((bf16[32,4,8,128]{3,2,1,0:T(8,128)(2,1)}), bf16[32,4,8,128]{3,2,1,0:T(8,128)(2,1)S(1)}, u32[]{:S(2)}, u32[]{:S(2)}) async-start(bf16[32,4,8,128]{3,2,1,0:T(8,128)(2,1)} %broadcast_select_fusion), calls=%async_computation | async-start | bytes 524288 | tf_op jit(solution)/shard_map/all_to_all | solution.py:24
  11.1 9.4 %collective-permute-start = (bf16[1,1024,2,128]{3,2,1,0:T(2,128)(2,1)}, bf16[1,1024,2,128]{3,2,1,0:T(2,128)(2,1)}, u32[]{:S(2)}, u32[]{:S(2)}) collective-permute-start(bf16[1,1024,2,128]{3,2,1,0:T(2,128)(2,1)} %param.19), channel_id=1, source_target_pairs={{0,4},{4,0},{1,5},{5,1},{2,6},{6,2},{3,7},{7,3},{8,12},{12,8},{9,1... | collective-permute-start | bytes 1572872 | tf_op jit(solution)/shard_map/ppermute | solution.py:28
  11.5 9.1 %collective-permute-start.1 = (bf16[1,1024,2,128]{3,2,1,0:T(2,128)(2,1)}, bf16[1,1024,2,128]{3,2,1,0:T(2,128)(2,1)}, u32[]{:S(2)}, u32[]{:S(2)}) collective-permute-start(bf16[1,1024,2,128]{3,2,1,0:T(2,128)(2,1)} %param.20), channel_id=1, source_target_pairs={{0,4},{4,0},{1,5},{5,1},{2,6},{6,2},{3,7},{7,3},{8,12},{12,8},{9,1... | collective-permute-start | bytes 1572872 | tf_op jit(solution)/shard_map/ppermute | solution.py:28
  11.7 3.3 %collective-permute-start.2 = (bf16[512,2,128]{2,1,0:T(2,128)(2,1)}, bf16[512,2,128]{2,1,0:T(2,128)(2,1)S(1)}, u32[]{:S(2)}, u32[]{:S(2)}) collective-permute-start(bf16[512,2,128]{2,1,0:T(2,128)(2,1)} %param.17), channel_id=1, source_target_pairs={{0,4},{4,0},{1,5},{5,1},{2,6},{6,2},{3,7},{7,3},{8,12},{12,8},{9,1... | collective-permute-start | bytes 786440 | tf_op jit(solution)/shard_map/ppermute | solution.py:28
  12.0 3.8 %collective-permute-start.3 = (bf16[512,2,128]{2,1,0:T(2,128)(2,1)}, bf16[512,2,128]{2,1,0:T(2,128)(2,1)S(1)}, u32[]{:S(2)}, u32[]{:S(2)}) collective-permute-start(bf16[512,2,128]{2,1,0:T(2,128)(2,1)} %param.18), channel_id=1, source_target_pairs={{0,4},{4,0},{1,5},{5,1},{2,6},{6,2},{3,7},{7,3},{8,12},{12,8},{9,1... | collective-permute-start | bytes 786440 | tf_op jit(solution)/shard_map/ppermute | solution.py:28
  15.0 0.7 copy-start.7
  15.7 0.7 copy-start.9
  16.4 0.9 copy-start.5
  17.4 0.9 copy-start.6
  18.3 0.9 copy-start.8
  19.3 0.9 copy-start.10
  20.6 12.4 %copy-start.18 = (s32[4]{0:T(128)S(1)}, s32[4]{0:T(128)}, u32[]{:S(2)}) copy-start(s32[4]{0:T(128)} %param.24) | copy-start | bytes 52
  25.8 8.8 %collective-permute-start.5 = (bf16[4,256,2,128]{3,2,1,0:T(2,128)(2,1)}, bf16[4,256,2,128]{3,2,1,0:T(2,128)(2,1)S(1)}, u32[]{:S(2)}, u32[]{:S(2)}) collective-permute-start(bf16[4,256,2,128]{3,2,1,0:T(2,128)(2,1)} %param.21), channel_id=1, source_target_pairs={{0,4},{4,0},{1,5},{5,1},{2,6},{6,2},{3,7},{7,3},{8,12},{12,8},{9,1... | collective-permute-start | bytes 1572872 | tf_op jit(solution)/shard_map/ppermute | solution.py:28
  26.0 8.6 %collective-permute-start.6 = (bf16[4,256,2,128]{3,2,1,0:T(2,128)(2,1)}, bf16[4,256,2,128]{3,2,1,0:T(2,128)(2,1)S(1)}, u32[]{:S(2)}, u32[]{:S(2)}) collective-permute-start(bf16[4,256,2,128]{3,2,1,0:T(2,128)(2,1)} %param.22), channel_id=1, source_target_pairs={{0,4},{4,0},{1,5},{5,1},{2,6},{6,2},{3,7},{7,3},{8,12},{12,8},{9,1... | collective-permute-start | bytes 1572872 | tf_op jit(solution)/shard_map/ppermute | solution.py:28
  26.3 15.5 %all-to-all-start.1 = ((bf16[16,80,128]{2,1,0:T(8,128)(2,1)}), bf16[16,80,128]{2,1,0:T(8,128)(2,1)S(1)}, u32[]{:S(2)}, u32[]{:S(2)}) async-start(bf16[16,80,128]{2,1,0:T(8,128)(2,1)} %shared_part.1), calls=%async_computation.1 | async-start | bytes 655360 | tf_op jit(solution)/shard_map/all_to_all | solution.py:24
  33.0 1.5 %collective-permute-start.4 = (s32[4]{0:T(128)S(1)}, s32[4]{0:T(128)S(1)}, u32[]{:S(2)}, u32[]{:S(2)}) collective-permute-start(s32[4]{0:T(128)S(1)} %copy-done.18), channel_id=1, source_target_pairs={{0,4},{4,0},{1,5},{5,1},{2,6},{6,2},{3,7},{7,3},{8,12},{12,8},{9,1... | collective-permute-start | bytes 56 | tf_op jit(solution)/shard_map/ppermute | solution.py:28
  43.5 11.0 %all-to-all-start.2 = ((bf16[16,8,1024]{2,1,0:T(8,128)(2,1)}), bf16[16,8,1024]{2,1,0:T(8,128)(2,1)S(1)}, u32[]{:S(2)}, u32[]{:S(2)}) async-start(bf16[16,8,1024]{2,1,0:T(8,128)(2,1)} %merged.1), calls=%async_computation.2 | async-start | bytes 524288 | tf_op jit(solution)/shard_map/all_to_all | solution.py:24
  52.2 16.5 %copy-start.15 = (bf16[128,256]{1,0:T(8,128)(2,1)S(1)}, bf16[128,256]{1,0:T(8,128)(2,1)}, u32[]{:S(2)}) copy-start(bf16[128,256]{1,0:T(8,128)(2,1)} %param.26) | copy-start | bytes 196612
  52.2 17.4 %copy-start.16 = (f32[256]{0:T(256)S(1)}, f32[256]{0:T(256)}, u32[]{:S(2)}) copy-start(f32[256]{0:T(256)} %param.27) | copy-start | bytes 3076
  54.6 3.8 %collective-permute-start.7 = (bf16[128,1024]{1,0:T(8,128)(2,1)S(1)}, bf16[128,1024]{1,0:T(8,128)(2,1)S(1)}, u32[]{:S(2)}, u32[]{:S(2)}) collective-permute-start(bf16[128,1024]{1,0:T(8,128)(2,1)S(1)} %bitcast.50), channel_id=1, source_target_pairs={{0,4},{4,0},{1,5},{5,1},{2,6},{6,2},{3,7},{7,3},{8,12},{12,8},{9,1... | collective-permute-start | bytes 786440 | tf_op jit(solution)/shard_map/ppermute | solution.py:28
  58.4 12.4 %collective-permute-start.13 = (bf16[512,3584]{1,0:T(8,128)(2,1)}, bf16[512,3584]{1,0:T(8,128)(2,1)}, u32[]{:S(2)}, u32[]{:S(2)}) collective-permute-start(bf16[512,3584]{1,0:T(8,128)(2,1)} %get-tuple-element.45), channel_id=1, source_target_pairs={{0,4},{4,0},{1,5},{5,1},{2,6},{6,2},{3,7},{7,3},{8,12},{12,8},{9,1... | collective-permute-start | bytes 11010056 | tf_op jit(solution)/shard_map/ppermute | solution.py:28
  59.3 4.1 %collective-permute-start.10 = (bf16[128,256]{1,0:T(8,128)(2,1)S(1)}, bf16[128,256]{1,0:T(8,128)(2,1)S(1)}, u32[]{:S(2)}, u32[]{:S(2)}) collective-permute-start(bf16[128,256]{1,0:T(8,128)(2,1)S(1)} %fusion), channel_id=1, source_target_pairs={{0,3},{1,0},{2,1},{3,2},{4,7},{5,4},{6,5},{7,6},{8,11},{9,8},{10,9... | collective-permute-start | bytes 196616 | tf_op jit(solution)/shard_map/ppermute | solution.py:470
  62.0 4.7 %collective-permute-start.9 = (bf16[128,256]{1,0:T(8,128)(2,1)S(1)}, bf16[128,256]{1,0:T(8,128)(2,1)S(1)}, u32[]{:S(2)}, u32[]{:S(2)}) collective-permute-start(bf16[128,256]{1,0:T(8,128)(2,1)S(1)} %fusion), channel_id=1, source_target_pairs={{0,2},{1,3},{2,0},{3,1},{4,6},{5,7},{6,4},{7,5},{8,10},{9,11},{10,... | collective-permute-start | bytes 196616 | tf_op jit(solution)/shard_map/ppermute | solution.py:470
  62.4 6.3 %collective-permute-start.8 = (bf16[128,256]{1,0:T(8,128)(2,1)S(1)}, bf16[128,256]{1,0:T(8,128)(2,1)S(1)}, u32[]{:S(2)}, u32[]{:S(2)}) collective-permute-start(bf16[128,256]{1,0:T(8,128)(2,1)S(1)} %fusion), channel_id=1, source_target_pairs={{0,1},{1,2},{2,3},{3,0},{4,5},{5,6},{6,7},{7,4},{8,9},{9,10},{10,1... | collective-permute-start | bytes 196616 | tf_op jit(solution)/shard_map/ppermute | solution.py:470
  68.7 2.0 %copy-start.13 = (f32[128,256]{1,0:T(8,128)}, f32[128,256]{1,0:T(8,128)S(1)}, u32[]{:S(2)}) copy-start(f32[128,256]{1,0:T(8,128)S(1)} %convert_add_fusion.near_ref) | copy-start | bytes 393220
  68.8 2.0 %collective-permute-start.11 = (f32[128,256]{1,0:T(8,128)S(1)}, f32[128,256]{1,0:T(8,128)S(1)}, u32[]{:S(2)}, u32[]{:S(2)}) collective-permute-start(f32[128,256]{1,0:T(8,128)S(1)} %convert_add_fusion.near_ref), channel_id=1, source_target_pairs={{0,4},{4,0},{1,5},{5,1},{2,6},{6,2},{3,7},{7,3},{8,12},{12,8},{9,1... | collective-permute-start | bytes 393224 | tf_op jit(solution)/shard_map/ppermute | solution.py:28
  69.6 1.1 collective-permute-start.12
  70.7 0.6 copy-start.17
  70.7 0.7 copy-start.14
  77.1 4.2 %collective-permute-start.14 = (bf16[3584,256]{1,0:T(8,128)(2,1)}, bf16[3584,256]{1,0:T(8,128)(2,1)}, u32[]{:S(2)}, u32[]{:S(2)}) collective-permute-start(bf16[3584,256]{1,0:T(8,128)(2,1)} %get-tuple-element.49), channel_id=1, source_target_pairs={{0,4},{4,0},{1,5},{5,1},{2,6},{6,2},{3,7},{7,3},{8,12},{12,8},{9,1... | collective-permute-start | bytes 5505032 | tf_op jit(solution)/shard_map/ppermute | solution.py:28
  77.4 33.5 %all-to-all-start.3 = ((bf16[16,8,7296]{2,1,0:T(8,128)(2,1)}), bf16[16,8,7296]{2,1,0:T(8,128)(2,1)S(1)}, u32[]{:S(2)}, u32[]{:S(2)}) async-start(bf16[16,8,7296]{2,1,0:T(8,128)(2,1)} %bitcast.49), calls=%async_computation.3 | async-start | bytes 3735552 | tf_op jit(solution)/shard_map/all_to_all | solution.py:24
  110.9 0.7 copy-start.11
  111.6 17.8 %copy-start.1 = (bf16[3584,256]{1,0:T(8,128)(2,1)S(1)}, bf16[3584,256]{1,0:T(8,128)(2,1)}, u32[]{:S(2)}) copy-start(bf16[3584,256]{1,0:T(8,128)(2,1)} %get-tuple-element.51.near) | copy-start | bytes 5505028
  111.6 17.8 %copy-start.2 = (bf16[3584,256]{1,0:T(8,128)(2,1)S(1)}, bf16[3584,256]{1,0:T(8,128)(2,1)}, u32[]{:S(2)}) copy-start(bf16[3584,256]{1,0:T(8,128)(2,1)} %get-tuple-element.52.far) | copy-start | bytes 5505028
